TPU v7x, 32 devices: a whole 2x2x4 slice. The times are simulated.
32 devices in a mesh: row: 4 (over y, x), col: 8 (over z, core).
Axes of the slice: x: 2, y: 2, z: 4, core: 2. Of those that a mesh axis runs over, the one named last changes fastest.
Arguments:
- tokens: bfloat16 [256, 8192], P('col', 'row'), may hold values from -500 to 500
- norm_gain: float32 [8192], P('row'), may hold values from 0.5 to 1.5
- cotangent: bfloat16 [256, 8192], P('col', 'row'), may hold values from -6 to 6
- gate_frozen_weight: bfloat16 [8192, 28672], P('row', 'col'), may hold values from -0.0625 to 0.0625
- up_frozen_weight: bfloat16 [8192, 28672], P('row', 'col'), may hold values from -0.0625 to 0.0625
- down_frozen_weight: bfloat16 [28672, 8192], P('col', 'row'), may hold values from -0.03125 to 0.03125
- gate_input_factor: bfloat16 [8192, 64], P('row'), may hold values from -0.0625 to 0.0625
- gate_output_factor: bfloat16 [64, 28672], P(None, 'col'), may hold values from -0.75 to 0.75
- up_input_factor: bfloat16 [8192, 64], P('row'), may hold values from -0.0625 to 0.0625
- up_output_factor: bfloat16 [64, 28672], P(None, 'col'), may hold values from -0.75 to 0.75
- down_input_factor: bfloat16 [28672, 64], P('col'), may hold values from -0.03125 to 0.03125
- down_b: bfloat16 [64, 8192], P(None, 'row'), may hold values from -0.75 to 0.75
- gate_input_factor_direction: bfloat16 [8192, 64], P('row'), may hold values from -0.0625 to 0.0625
- gate_output_factor_direction: bfloat16 [64, 28672], P(None, 'col'), may hold values from -0.75 to 0.75
- up_input_factor_direction: bfloat16 [8192, 64], P('row'), may hold values from -0.0625 to 0.0625
- up_output_factor_direction: bfloat16 [64, 28672], P(None, 'col'), may hold values from -0.75 to 0.75
- down_input_factor_direction: bfloat16 [28672, 64], P('col'), may hold values from -0.03125 to 0.03125
- down_b_dir: bfloat16 [64, 8192], P(None, 'row'), may hold values from -0.75 to 0.75
Outputs:
- normed_feature_adjoint: float32 [256, 8192], P('col', 'row')
- normed_feature_adjoint_direction: float32 [256, 8192], P('col', 'row')
- curvature_gate_input: float32 [8192, 64], P('row')
- curvature_gate_output: float32 [64, 28672], P(None, 'col')
- curvature_up_input: float32 [8192, 64], P('row')
- curvature_up_output: float32 [64, 28672], P(None, 'col')
- curvature_down_input: float32 [28672, 64], P('col')
- curvature_down_output: float32 [64, 8192], P(None, 'row')
All inputs are finite; a program needn't handle non-finite values.
Results may differ from a plain program's by a relative error of at most 0.024.
Values may be sent and summed in bfloat16 or wider, within the bound.
A program may use at most 128 MiB of HBM per device.

v0:
```python
import functools

import jax
import jax.numpy as jnp
from jax import lax
from jax.experimental import pallas as pl
from jax.experimental.pallas import tpu as pltpu
from jax.sharding import PartitionSpec as P

adapter_scale = 0.5
epsilon = 1e-05
MESH = pl.DeviceIdType.MESH


def total_kernel(axis, n, x_ref, o_ref, inbox, whole, send1, recv1, send2, recv2):
    me = lax.axis_index(axis)
    barrier = pltpu.get_barrier_semaphore()

    @pl.loop(1, n)
    def _(k):
        pl.semaphore_signal(
            barrier, inc=1, device_id={axis: lax.rem(me + k, n)}, device_id_type=MESH
        )

    pl.semaphore_wait(barrier, n - 1)

    def scatter(k):
        peer = lax.rem(me + k, n)
        return pltpu.make_async_remote_copy(
            src_ref=x_ref.at[peer],
            dst_ref=inbox.at[k],
            send_sem=send1.at[k],
            recv_sem=recv1.at[k],
            device_id={axis: peer},
            device_id_type=MESH,
        )

    def spread(k):
        peer = lax.rem(me + k, n)
        return pltpu.make_async_remote_copy(
            src_ref=whole.at[me],
            dst_ref=whole.at[me],
            send_sem=send2.at[k],
            recv_sem=recv2.at[k],
            device_id={axis: peer},
            device_id_type=MESH,
        )

    def arrival(k):
        origin = lax.rem(me - k + n, n)
        return pltpu.make_async_remote_copy(
            src_ref=whole.at[origin],
            dst_ref=whole.at[origin],
            send_sem=send2.at[k],
            recv_sem=recv2.at[k],
            device_id={axis: origin},
            device_id_type=MESH,
        )

    @pl.loop(1, n)
    def _(k):
        scatter(k).start()

    def add(k, total):
        scatter(k).wait_recv()
        return total + inbox[k].astype(jnp.float32)

    total = lax.fori_loop(1, n, add, x_ref[me].astype(jnp.float32))
    whole[me] = total.astype(whole.dtype)

    @pl.loop(1, n)
    def _(k):
        spread(k).start()

    @pl.loop(1, n)
    def _(k):
        arrival(k).wait_recv()

    @pl.loop(1, n)
    def _(k):
        scatter(k).wait_send()
        spread(k).wait_send()

    o_ref[...] = whole[...]


def shard_total(x, axis, collective_id):
    n = lax.axis_size(axis)
    rows, columns = x.shape
    block = (n, rows // n, columns)
    total = pl.pallas_call(
        functools.partial(total_kernel, axis, n),
        out_shape=jax.ShapeDtypeStruct(block, jnp.bfloat16),
        in_specs=[pl.BlockSpec(memory_space=pltpu.VMEM)],
        out_specs=pl.BlockSpec(memory_space=pltpu.VMEM),
        scratch_shapes=[
            pltpu.VMEM(block, x.dtype),
            pltpu.VMEM(block, jnp.bfloat16),
            pltpu.SemaphoreType.DMA((n,)),
            pltpu.SemaphoreType.DMA((n,)),
            pltpu.SemaphoreType.DMA((n,)),
            pltpu.SemaphoreType.DMA((n,)),
        ],
        compiler_params=pltpu.CompilerParams(collective_id=collective_id, has_side_effects=True),
        name=f"total_{axis}",
    )(x.reshape(block))
    return total.reshape(rows, columns)


def curvature_product(left, right):
    return jnp.dot(left, right, preferred_element_type=jnp.float32)


def cross_shard_total(left, right):
    return lax.dot_general(
        left, right, (((1,), (1,)), ((), ())), preferred_element_type=jnp.float32
    )


def summed_over_rows(left, right):
    return lax.dot_general(
        left, right, (((0,), (0,)), ((), ())), preferred_element_type=jnp.float32
    )


def second_order(
    gate_preactivation,
    up_preactivation,
    hidden_adjoint,
    gate_tangent_rows,
    up_tangent_rows,
    adjoint_tangent_rows,
):
    sigma = jax.nn.sigmoid(gate_preactivation)
    silu_value = gate_preactivation * sigma
    slope = sigma * (1.0 + gate_preactivation * (1.0 - sigma))
    bend = sigma * (1.0 - sigma) * (2.0 + gate_preactivation * (1.0 - 2.0 * sigma))
    hidden_activation = (silu_value * up_preactivation).astype(jnp.bfloat16)
    hidden_direction = (
        slope * gate_tangent_rows * up_preactivation + silu_value * up_tangent_rows
    ).astype(jnp.bfloat16)
    gate_derivative = (hidden_adjoint * up_preactivation * slope).astype(jnp.bfloat16)
    up_derivative = (hidden_adjoint * silu_value).astype(jnp.bfloat16)
    gate_derivative_direction = (
        adjoint_tangent_rows * up_preactivation * slope
        + hidden_adjoint * (up_tangent_rows * slope + up_preactivation * bend * gate_tangent_rows)
    ).astype(jnp.bfloat16)
    up_derivative_direction = (
        adjoint_tangent_rows * silu_value + hidden_adjoint * slope * gate_tangent_rows
    ).astype(jnp.bfloat16)
    return (
        hidden_activation,
        hidden_direction,
        gate_derivative,
        up_derivative,
        gate_derivative_direction,
        up_derivative_direction,
    )


def block_kernel(
    x_ref,
    cot_ref,
    gate_hbm,
    up_hbm,
    down_hbm,
    gate_left,
    up_left,
    adj_left,
    gate_stack,
    up_stack,
    adj_stack,
    gate_out,
    up_out,
    down_in,
    feature_ref,
    gate_q,
    up_q,
    low_q,
    gate_curve,
    up_curve,
    down_curve,
    parts,
    first_in,
    second_out,
    second_in,
    whole,
    wide_buf,
    down_buf,
    total,
    send_sem,
    recv_sem,
    wide_sem,
    down_sem,
):
    me = lax.axis_index("row")
    flip_low = me + 1 - 2 * lax.rem(me, 2)
    flip_high = me + 2 - 4 * (me // 2)
    flip_both = 3 - me
    chunks, blocks, block, triple = parts.shape
    width = triple // 3
    count = x_ref.shape[0]
    depth = x_ref.shape[1]
    slots = wide_buf.shape[0]

    barrier = pltpu.get_barrier_semaphore()
    for peer in (flip_low, flip_high):
        pl.semaphore_signal(barrier, inc=1, device_id={"row": peer}, device_id_type=MESH)

    def lanes(c):
        return pl.ds(pl.multiple_of(c * width, width), width)

    def loads(c):
        slot, side = lax.rem(c, slots), lax.rem(c, 2)
        return [
            pltpu.make_async_copy(
                gate_hbm.at[:, lanes(c)], wide_buf.at[slot, 0], wide_sem.at[slot, 0]
            ),
            pltpu.make_async_copy(
                up_hbm.at[:, lanes(c)], wide_buf.at[slot, 1], wide_sem.at[slot, 1]
            ),
            pltpu.make_async_copy(down_hbm.at[lanes(c), :], down_buf.at[side], down_sem.at[side]),
        ]

    def send(src, dst, c, path, k, peer):
        return pltpu.make_async_remote_copy(
            src_ref=src,
            dst_ref=dst,
            send_sem=send_sem.at[c, path, k],
            recv_sem=recv_sem.at[c, path, k],
            device_id={"row": peer},
            device_id_type=MESH,
        )

    def ends(path):
        return (flip_low, flip_high) if path == 0 else (flip_high, flip_low)

    def sends(c, path, ks):
        near, far = ends(path)
        base = 4 * path
        table = [
            lambda: send(parts.at[c, base + near], first_in.at[c, path, 0], c, path, 0, near),
            lambda: send(parts.at[c, base + flip_both], first_in.at[c, path, 1], c, path, 1, near),
            lambda: send(second_out.at[c, path], second_in.at[c, path], c, path, 2, far),
            lambda: send(whole.at[c, base + me], whole.at[c, base + me], c, path, 3, far),
            lambda: send(whole.at[c, base + me], whole.at[c, base + me], c, path, 4, near),
            lambda: send(whole.at[c, base + far], whole.at[c, base + far], c, path, 5, near),
        ]
        return [table[k]() for k in ks]

    def arrivals(c, path, ks):
        near, far = ends(path)
        base = 4 * path
        table = [
            lambda: send(parts.at[c, base + me], first_in.at[c, path, 0], c, path, 0, near),
            lambda: send(parts.at[c, base + far], first_in.at[c, path, 1], c, path, 1, near),
            lambda: send(second_out.at[c, path], second_in.at[c, path], c, path, 2, far),
            lambda: send(whole.at[c, base + far], whole.at[c, base + far], c, path, 3, far),
            lambda: send(whole.at[c, base + near], whole.at[c, base + near], c, path, 4, near),
            lambda: send(whole.at[c, base + flip_both], whole.at[c, base + flip_both], c, path, 5, near),
        ]
        return [table[k]() for k in ks]

    def put(c, at, value):
        parts[c, :, :, at * width : (at + 1) * width] = value.astype(jnp.bfloat16).reshape(
            blocks, block, width
        )

    for copy in loads(0):
        copy.start()
    total[...] = jnp.zeros_like(total)
    gate_q[...] = jnp.zeros_like(gate_q)
    up_q[...] = jnp.zeros_like(up_q)
    low_q[...] = jnp.zeros_like(low_q)
    pl.semaphore_wait(barrier, 2)

    def project(c):
        for copy in loads(c):
            copy.wait()

        @pl.when(c + 1 < chunks)
        def _():
            for copy in loads(c + 1):
                copy.start()

        slot = lax.rem(c, slots)
        put(c, 0, curvature_product(x_ref[...], wide_buf[slot, 0]))
        put(c, 1, curvature_product(x_ref[...], wide_buf[slot, 1]))
        put(c, 2, cross_shard_total(cot_ref[...], down_buf[lax.rem(c, 2)]))
        for path in range(2):
            for copy in sends(c, path, (0, 1)):
                copy.start()

    def relay(c):
        for path in range(2):
            near, far = ends(path)
            for copy in arrivals(c, path, (0, 1)):
                copy.wait_recv()
            second_out[c, path] = (
                parts[c, 4 * path + far].astype(jnp.float32)
                + first_in[c, path, 1].astype(jnp.float32)
            ).astype(jnp.bfloat16)
            sends(c, path, (2,))[0].start()

    def settle(c):
        for path in range(2):
            arrivals(c, path, (2,))[0].wait_recv()
            whole[c, 4 * path + me] = (
                parts[c, 4 * path + me].astype(jnp.float32)
                + first_in[c, path, 0].astype(jnp.float32)
                + second_in[c, path].astype(jnp.float32)
            ).astype(jnp.bfloat16)
            for copy in sends(c, path, (3, 4)):
                copy.start()

    def forward(c):
        for path in range(2):
            arrivals(c, path, (3,))[0].wait_recv()
            sends(c, path, (5,))[0].start()

    def differentiate(c):
        for path in range(2):
            for copy in arrivals(c, path, (4, 5)):
                copy.wait_recv()

        def got(at):
            return (
                whole[c, :, :, at * width : (at + 1) * width]
                .reshape(count, width)
                .astype(jnp.float32)
            )

        gate_w, up_w, down_w = gate_out[:, lanes(c)], up_out[:, lanes(c)], down_in[lanes(c), :]
        gate_low = curvature_product(gate_left[...], gate_w)
        up_low = curvature_product(up_left[...], up_w)
        adj_low = cross_shard_total(adj_left[...], down_w)
        hidden, hidden_dir, d_gate, d_up, d_gate_dir, d_up_dir = second_order(
            got(0) + gate_low[:count],
            got(1) + up_low[:count],
            got(2) + adj_low[:count],
            gate_low[count:],
            up_low[count:],
            adj_low[count:],
        )
        gate_d = jnp.concatenate([d_gate, d_gate_dir], axis=0)
        up_d = jnp.concatenate([d_up, d_up_dir], axis=0)
        hidden_d = jnp.concatenate([hidden_dir, hidden], axis=0)
        gate_curve[:, lanes(c)] = curvature_product(gate_stack[...], gate_d)
        up_curve[:, lanes(c)] = curvature_product(up_stack[...], up_d)
        down_curve[:, lanes(c)] = curvature_product(adj_stack[...], hidden_d)
        gate_q[...] += cross_shard_total(gate_d, gate_w)
        up_q[...] += cross_shard_total(up_d, up_w)
        low_q[...] += curvature_product(hidden_d, down_w)
        slot = lax.rem(c, slots)
        piece = 512 if depth % 512 == 0 else depth
        for start in range(0, depth, piece):
            span = slice(start, start + piece)
            total[:, span] += cross_shard_total(
                gate_d, wide_buf[slot, 0, span, :]
            ) + cross_shard_total(up_d, wide_buf[slot, 1, span, :])

    @pl.loop(0, chunks + 4)
    def _(t):
        for lag, stage in enumerate((project, relay, settle, forward, differentiate)):

            @pl.when((t >= lag) & (t < chunks + lag))
            def _(lag=lag, stage=stage):
                stage(t - lag)

    @pl.loop(0, chunks)
    def _(c):
        for path in range(2):
            for copy in sends(c, path, range(6)):
                copy.wait_send()

    feature_ref[...] = total[...].astype(jnp.bfloat16)


def fused_block(x, cot, gate_w, up_w, down_w, ranks, gate_out, up_out, down_in, width):
    count, depth = x.shape
    columns = gate_w.shape[1]
    rank = ranks.shape[1] // 6
    chunks = columns // width
    half = ranks * adapter_scale
    gate, up, gate_dir, up_dir, adj, adj_dir = [
        half[:, index * rank : (index + 1) * rank] for index in range(6)
    ]
    empty = jnp.zeros_like(gate)

    def left(low, low_dir):
        return jnp.concatenate(
            [
                jnp.concatenate([low, empty], axis=1),
                jnp.concatenate([low_dir, low], axis=1),
            ],
            axis=0,
        )

    vmem = pl.BlockSpec(memory_space=pltpu.VMEM)
    anywhere = pl.BlockSpec(memory_space=pl.ANY)
    block = count // 8
    f32, bf16 = jnp.float32, jnp.bfloat16
    return pl.pallas_call(
        block_kernel,
        out_shape=[
            jax.ShapeDtypeStruct((2 * count, depth), bf16),
            jax.ShapeDtypeStruct((2 * count, 2 * rank), f32),
            jax.ShapeDtypeStruct((2 * count, 2 * rank), f32),
            jax.ShapeDtypeStruct((2 * count, 2 * rank), f32),
            jax.ShapeDtypeStruct((rank, columns), f32),
            jax.ShapeDtypeStruct((rank, columns), f32),
            jax.ShapeDtypeStruct((rank, columns), f32),
        ],
        in_specs=[vmem] * 2 + [anywhere] * 3 + [vmem] * 9,
        out_specs=[vmem] * 7,
        scratch_shapes=[
            pltpu.VMEM((chunks, 8, block, 3 * width), bf16),
            pltpu.VMEM((chunks, 2, 2, block, 3 * width), bf16),
            pltpu.VMEM((chunks, 2, block, 3 * width), bf16),
            pltpu.VMEM((chunks, 2, block, 3 * width), bf16),
            pltpu.VMEM((chunks, 8, block, 3 * width), bf16),
            pltpu.VMEM((6, 2, depth, width), bf16),
            pltpu.VMEM((2, width, depth), bf16),
            pltpu.VMEM((2 * count, depth), f32),
            pltpu.SemaphoreType.DMA((chunks, 2, 6)),
            pltpu.SemaphoreType.DMA((chunks, 2, 6)),
            pltpu.SemaphoreType.DMA((6, 2)),
            pltpu.SemaphoreType.DMA((2,)),
        ],
        compiler_params=pltpu.CompilerParams(
            collective_id=2, has_side_effects=True, vmem_limit_bytes=60 * 1024 * 1024
        ),
        name="block",
    )(
        x,
        cot,
        gate_w,
        up_w,
        down_w,
        left(gate, gate_dir),
        left(up, up_dir),
        left(adj, adj_dir),
        jnp.concatenate([gate_dir, gate], axis=0).T,
        jnp.concatenate([up_dir, up], axis=0).T,
        jnp.concatenate([adj, adj_dir], axis=0).T,
        gate_out,
        up_out,
        down_in,
    )


def gather_kernel(
    tokens,
    gain,
    cot,
    x_all,
    cot_all,
    x_buf,
    cot_buf,
    squares,
    square_send,
    square_recv,
    far_send,
    far_recv,
    near_send,
    near_recv,
):
    rows, columns = lax.axis_size("row"), lax.axis_size("col")
    chips = columns // 2
    my_row, me = lax.axis_index("row"), lax.axis_index("col")
    partner = me + 1 - 2 * lax.rem(me, 2)
    features = rows * tokens.shape[1]
    barrier = pltpu.get_barrier_semaphore()

    def row_peer(k):
        return {"row": lax.rem(my_row + k, rows)}

    def far_peer(k):
        return {"col": lax.rem(me + 2 * k, columns)}

    @pl.loop(1, rows)
    def _(k):
        pl.semaphore_signal(barrier, inc=1, device_id=row_peer(k), device_id_type=MESH)

    @pl.loop(1, chips)
    def _(k):
        pl.semaphore_signal(barrier, inc=1, device_id=far_peer(k), device_id_type=MESH)

    pl.semaphore_signal(barrier, inc=1, device_id={"col": partner}, device_id_type=MESH)

    buffers = (cot_buf, x_buf)

    def origin(k):
        return lax.rem(me - 2 * k + columns, columns)

    def square(k):
        return pltpu.make_async_remote_copy(
            src_ref=squares.at[0],
            dst_ref=squares.at[k],
            send_sem=square_send.at[k],
            recv_sem=square_recv.at[k],
            device_id=row_peer(k),
            device_id_type=MESH,
        )

    def far(which, k, slot):
        return pltpu.make_async_remote_copy(
            src_ref=buffers[which].at[slot],
            dst_ref=buffers[which].at[slot],
            send_sem=far_send.at[which, k],
            recv_sem=far_recv.at[which, k],
            device_id=far_peer(k),
            device_id_type=MESH,
        )

    def near(which, k, slot):
        return pltpu.make_async_remote_copy(
            src_ref=buffers[which].at[slot],
            dst_ref=buffers[which].at[slot],
            send_sem=near_send.at[which, k],
            recv_sem=near_recv.at[which, k],
            device_id={"col": partner},
            device_id_type=MESH,
        )

    def launch(which):
        @pl.loop(1, chips)
        def _(k):
            far(which, k, me).start()

        near(which, 0, me).start()

    values = tokens[...].astype(jnp.float32)
    squares[0] = jnp.broadcast_to(
        jnp.sum(values * values, axis=1, keepdims=True), squares.shape[1:]
    )
    cot_buf[me] = cot[...]
    pl.semaphore_wait(barrier, rows + chips - 1)

    @pl.loop(1, rows)
    def _(k):
        square(k).start()

    launch(0)

    def add(k, total):
        square(k).wait_recv()
        return total + squares[k]

    total = lax.fori_loop(1, rows, add, squares[0])
    scale = lax.rsqrt(total[:, :1] / features + epsilon)
    x_buf[me] = (tokens[...].astype(jnp.float32) * scale * gain[...]).astype(jnp.bfloat16)
    launch(1)
    for which in range(2):

        @pl.loop(1, chips)
        def _(k, which=which):
            far(which, k, origin(k)).wait_recv()
            near(which, k, origin(k)).start()

    for which in range(2):

        @pl.loop(0, chips)
        def _(k, which=which):
            near(which, k, lax.rem(partner - 2 * k + columns, columns)).wait_recv()

    @pl.loop(1, rows)
    def _(k):
        square(k).wait_send()

    for which in range(2):

        @pl.loop(1, chips)
        def _(k, which=which):
            far(which, k, me).wait_send()

        @pl.loop(0, chips)
        def _(k, which=which):
            near(which, k, origin(k)).wait_send()

    cot_all[...] = cot_buf[...]
    x_all[...] = x_buf[...]


def gathered(tokens, gain, cot):
    rows, columns = lax.axis_size("row"), lax.axis_size("col")
    own, depth = tokens.shape
    whole = (columns, own, depth)
    vmem = pl.BlockSpec(memory_space=pltpu.VMEM)
    x, panel = pl.pallas_call(
        gather_kernel,
        out_shape=[jax.ShapeDtypeStruct(whole, jnp.bfloat16)] * 2,
        in_specs=[vmem] * 3,
        out_specs=[vmem] * 2,
        scratch_shapes=[
            pltpu.VMEM(whole, jnp.bfloat16),
            pltpu.VMEM(whole, jnp.bfloat16),
            pltpu.VMEM((rows, own, 128), jnp.float32),
            pltpu.SemaphoreType.DMA((rows,)),
            pltpu.SemaphoreType.DMA((rows,)),
            pltpu.SemaphoreType.DMA((2, columns // 2)),
            pltpu.SemaphoreType.DMA((2, columns // 2)),
            pltpu.SemaphoreType.DMA((2, columns // 2)),
            pltpu.SemaphoreType.DMA((2, columns // 2)),
        ],
        compiler_params=pltpu.CompilerParams(collective_id=3, has_side_effects=True),
        name="gather",
    )(tokens, gain.reshape(1, depth), cot)
    return x.reshape(columns * own, depth), panel.reshape(columns * own, depth)


def chunk_count(width):
    for count in (4, 2):
        if width % (128 * count) == 0:
            return count
    return 1


def on_device(
    tokens,
    norm_gain,
    cotangent,
    gate_frozen_weight,
    up_frozen_weight,
    down_frozen_weight,
    gate_input_factor,
    gate_output_factor,
    up_input_factor,
    up_output_factor,
    down_input_factor,
    down_b,
    gate_input_factor_direction,
    gate_output_factor_direction,
    up_input_factor_direction,
    up_output_factor_direction,
    down_input_factor_direction,
    down_b_dir,
):
    rank = gate_input_factor.shape[1]
    width_rows, width_columns = gate_frozen_weight.shape
    own_count = tokens.shape[0]
    normed_tokens, cot_panel = gathered(tokens, norm_gain, cotangent)
    count = normed_tokens.shape[0]
    in_factors = jnp.concatenate(
        [
            gate_input_factor,
            up_input_factor,
            gate_input_factor_direction,
            up_input_factor_direction,
        ],
        axis=1,
    )
    out_factors = jnp.concatenate([down_b, down_b_dir], axis=0)

    projected = jnp.concatenate(
        [curvature_product(normed_tokens, in_factors), cross_shard_total(cot_panel, out_factors)],
        axis=1,
    )
    ranks = shard_total(projected, "row", 0)
    gate_out = jnp.concatenate([gate_output_factor, gate_output_factor_direction], axis=0)
    up_out = jnp.concatenate([up_output_factor, up_output_factor_direction], axis=0)
    down_in = jnp.concatenate([down_input_factor, down_input_factor_direction], axis=1)

    width = 256
    if lax.axis_size("row") == 4 and width_columns % width == 0 and count % 128 == 0:
        feature, gate_q, up_q, low_q, gate_output, up_output, down_input = fused_block(
            normed_tokens,
            cot_panel,
            gate_frozen_weight,
            up_frozen_weight,
            down_frozen_weight,
            ranks,
            gate_out,
            up_out,
            down_in,
            width,
        )
        low_dir = low_q[:count, :rank] + low_q[count:, rank:]
        down_input = down_input.T
    else:
        chunks = chunk_count(width_columns)
        wide = width_columns // chunks
        spans = [slice(index * wide, (index + 1) * wide) for index in range(chunks)]

        summed_chunks = []
        for span in spans:
            partial = (
                curvature_product(normed_tokens, gate_frozen_weight[:, span]).astype(jnp.bfloat16),
                curvature_product(normed_tokens, up_frozen_weight[:, span]).astype(jnp.bfloat16),
                cross_shard_total(cot_panel, down_frozen_weight[span]).astype(jnp.bfloat16),
            )
            if summed_chunks:
                partial, summed_chunks[-1] = lax.optimization_barrier((partial, summed_chunks[-1]))
            summed_chunks.append(lax.psum(partial, "row"))

        gate_low, up_low, gate_low_dir, up_low_dir, adj_low, adj_low_dir = [
            ranks[:, index * rank : (index + 1) * rank] for index in range(6)
        ]
        gate_pair = jnp.concatenate([gate_low_dir, gate_low], axis=1)
        up_pair = jnp.concatenate([up_low_dir, up_low], axis=1)
        adj_pair = jnp.concatenate([adj_low_dir, adj_low], axis=1)
        gate_stack = jnp.concatenate([gate_low_dir, gate_low], axis=0)
        up_stack = jnp.concatenate([up_low_dir, up_low], axis=0)
        adj_stack = jnp.concatenate([adj_low, adj_low_dir], axis=0)
        feature = 0.0
        gate_q = 0.0
        up_q = 0.0
        low_dir = 0.0
        gate_output, up_output, down_input = [], [], []
        for span, total in zip(spans, summed_chunks):
            gate_sum, up_sum, adj_sum = [value.astype(jnp.float32) for value in total]
            gate_pre = gate_sum + adapter_scale * curvature_product(
                gate_low, gate_output_factor[:, span]
            )
            up_pre = up_sum + adapter_scale * curvature_product(
                up_low, up_output_factor[:, span]
            )
            hidden_adj = adj_sum + adapter_scale * cross_shard_total(
                adj_low, down_input_factor[span]
            )
            gate_tan = adapter_scale * curvature_product(gate_pair, gate_out[:, span])
            up_tan = adapter_scale * curvature_product(up_pair, up_out[:, span])
            adj_tan = adapter_scale * cross_shard_total(adj_pair, down_in[span])
            hidden, hidden_dir, d_gate, d_up, d_gate_dir, d_up_dir = second_order(
                gate_pre, up_pre, hidden_adj, gate_tan, up_tan, adj_tan
            )
            gate_d = jnp.concatenate([d_gate, d_gate_dir], axis=0)
            up_d = jnp.concatenate([d_up, d_up_dir], axis=0)
            hidden_d = jnp.concatenate([hidden_dir, hidden], axis=0)
            gate_output.append(adapter_scale * summed_over_rows(gate_stack, gate_d))
            up_output.append(adapter_scale * summed_over_rows(up_stack, up_d))
            down_input.append(adapter_scale * summed_over_rows(hidden_d, adj_stack))
            gate_q = gate_q + cross_shard_total(gate_d, gate_out[:, span])
            up_q = up_q + cross_shard_total(up_d, up_out[:, span])
            low_dir = (
                low_dir
                + curvature_product(hidden_dir, down_input_factor[span])
                + curvature_product(hidden, down_input_factor_direction[span])
            )
            feature = (
                feature
                + cross_shard_total(gate_d, gate_frozen_weight[:, span])
                + cross_shard_total(up_d, up_frozen_weight[:, span])
            )
        gate_output = jnp.concatenate(gate_output, axis=1)
        up_output = jnp.concatenate(up_output, axis=1)
        down_input = jnp.concatenate(down_input, axis=0)

    summed = lax.psum_scatter(
        feature.astype(jnp.bfloat16).reshape(2, count, width_rows),
        "col",
        scatter_dimension=1,
        tiled=True,
    ).astype(jnp.float32)
    adjoints = shard_total(
        jnp.concatenate(
            [
                gate_q[:count, :rank],
                up_q[:count, :rank],
                gate_q[count:, :rank] + gate_q[:count, rank:],
                up_q[count:, :rank] + up_q[:count, rank:],
                low_dir,
            ],
            axis=1,
        ).astype(jnp.bfloat16),
        "col",
        1,
    )
    piece = lax.dynamic_slice_in_dim(adjoints, lax.axis_index("col") * own_count, own_count, 0)
    normed_feature_adjoint = summed[0] + adapter_scale * cross_shard_total(
        piece[:, : 2 * rank], in_factors[:, : 2 * rank]
    )
    normed_feature_adjoint_direction = summed[1] + adapter_scale * cross_shard_total(
        jnp.concatenate([piece[:, 2 * rank : 4 * rank], piece[:, : 2 * rank]], axis=1), in_factors
    )
    gate_input = adapter_scale * summed_over_rows(
        normed_tokens, adjoints[:, 2 * rank : 3 * rank]
    )
    up_input = adapter_scale * summed_over_rows(normed_tokens, adjoints[:, 3 * rank : 4 * rank])
    down_output = adapter_scale * summed_over_rows(adjoints[:, 4 * rank :], cot_panel)
    return (
        normed_feature_adjoint,
        normed_feature_adjoint_direction,
        gate_input,
        gate_output,
        up_input,
        up_output,
        down_input,
        down_output,
    )


def solution(mesh):
    in_specs = (
        P("col", "row"),
        P("row"),
        P("col", "row"),
        P("row", "col"),
        P("row", "col"),
        P("col", "row"),
        P("row", None),
        P(None, "col"),
        P("row", None),
        P(None, "col"),
        P("col", None),
        P(None, "row"),
        P("row", None),
        P(None, "col"),
        P("row", None),
        P(None, "col"),
        P("col", None),
        P(None, "row"),
    )
    out_specs = (
        P("col", "row"),
        P("col", "row"),
        P("row", None),
        P(None, "col"),
        P("row", None),
        P(None, "col"),
        P("col", None),
        P(None, "row"),
    )
    return jax.shard_map(
        on_device, mesh=mesh, in_specs=in_specs, out_specs=out_specs, check_vma=False
    )
```

profile of v0, /device:TPU:0, one launch (start us, length us, event | category | flops | bytes accessed | tf_op | source)
XLA Modules:
  0.0 230.6 jit_solution(12443555470315412483)
XLA Ops:
  7.2 1.0 constant_dynamic-update-slice_fusion.3
  8.2 1.0 constant_dynamic-update-slice_fusion.2
  9.2 1.0 constant_dynamic-update-slice_fusion.1
  10.2 1.0 constant_dynamic-update-slice_fusion
  11.2 31.6 %gather.1 = (bf16[8,32,2048]{2,1,0:T(8,128)(2,1)}, bf16[8,32,2048]{2,1,0:T(8,128)(2,1)}) custom-call(bf16[32,2048]{1,0:T(8,128)(2,1)} %tokens.1, f32[1,2048]{1,0:T(1,128)} %bitcast.56, bf16[32,2048]{1,0:T(8,128)(2,1)} %cot.1), custom_call_target="tpu_custom_call" | custom-call | tf_op jit(solution)/shard_map/gather/pallas_call | solution.py:590
  42.8 1.8 fusion.24
  44.6 0.5 fusion.2
  45.1 0.9 copy.33
  46.1 13.2 %total_row.1 = bf16[4,64,384]{2,1,0:T(8,128)(2,1)} custom-call(f32[4,64,384]{2,1,0:T(8,128)} %bitcast.45), custom_call_target="tpu_custom_call" | custom-call | tf_op jit(solution)/shard_map/total_row/pallas_call | solution.py:91
  59.3 1.0 broadcast_multiply_fusion
  60.3 0.1 fusion.23
  60.4 0.1 copy.51
  60.5 0.1 copy.52
  60.6 0.6 maximum_bitcast_fusion.2.adj_stack
  61.2 0.1 copy.49
  61.3 0.1 copy.50
  61.4 0.6 maximum_bitcast_fusion.1.up_stack
  62.1 0.1 copy.47
  62.2 0.1 copy.48
  62.3 0.1 copy.46
  62.4 0.1 broadcast_select_fusion
  62.5 0.6 maximum_bitcast_fusion.gate_stack
  63.1 0.8 copy.43.gate_left
  63.9 0.8 copy.45.adj_left
  64.7 0.8 copy.44.up_left
  65.4 0.4 copy.41
  65.9 1.5 copy.42
  67.4 1.4 pad_maximum_fusion.2.down_in
  68.8 1.0 pad_maximum_fusion.gate_out
  69.8 1.0 pad_maximum_fusion.1.up_out
  70.8 106.1 %block.1 = (bf16[512,2048]{1,0:T(8,128)(2,1)}, f32[512,128]{1,0:T(8,128)}, f32[512,128]{1,0:T(8,128)}, f32[512,128]{1,0:T(8,128)}, f32[64,3584]{1,0:T(8,128)}, /*index=5*/f32[64,3584]{1,0:T(8,128)}, f32[64,3584]{1,0:T(8,128)}) custom-call(bf16[256,2048]{1,0:T(8,128)(2,1)} %bitcast.36, bf16[256,2048]{1,0:T(8,128)(2,1)} %bitcast.39, ...), custom_call_target="tpu_custom_call" | custom-call | tf_op jit(solution)/shard_map/block/pallas_call | solution.py:403
  177.0 1.6 slice.128
  178.6 0.6 slice.127
  179.2 1.2 add_convert_fusion.2
  180.4 1.7 add_convert_fusion
  182.1 1.7 concatenate.98.x_ref
  183.8 20.1 %total_col.1 = bf16[8,32,320]{2,1,0:T(8,128)(2,1)} custom-call(bf16[8,32,320]{2,1,0:T(8,128)(2,1)} %concatenate.98.x_ref), custom_call_target="tpu_custom_call" | custom-call | tf_op jit(solution)/shard_map/total_col/pallas_call | solution.py:91
  203.9 0.7 fusion.22
  204.7 2.0 convolution_multiply_fusion
  206.6 2.1 convolution_multiply_fusion.1
  208.7 2.0 convolution_multiply_fusion.2
  210.7 7.3 %reduce-scatter.2.cloned.1.call-done = bf16[2,32,2048]{2,1,0:T(8,128)(2,1)} async-done(((bf16[2,256,2048]{2,1,0:T(8,128)(2,1)}), bf16[2,32,2048]{2,1,0:T(8,128)(2,1)}) %reduce-scatter.2.cloned.1.call-update) | async-done | bytes 262160 | tf_op jit(solution)/shard_map/reduce_scatter | solution.py:749
  218.0 1.0 convert_element_type.5
  219.1 0.9 fusion.1
  220.0 1.0 fusion
  221.0 0.9 copy.59
  221.9 0.9 copy.60
  222.8 0.9 copy.61
  (41 shorter events, 0.2 us)
Async XLA Ops:
  7.2 210.9 %reduce-scatter.2.cloned.1.call-start = ((), (), s32[]{:S(2)}) async-start(), calls=%async_computation.1 | async-start | bytes 2359296 | tf_op jit(solution)/shard_map/reduce_scatter | solution.py:749
  9.2 35.4 %copy-start.15 = (bf16[64,2048]{1,0:T(8,128)(2,1)S(1)}, bf16[64,2048]{1,0:T(8,128)(2,1)}, u32[]{:S(2)}) copy-start(bf16[64,2048]{1,0:T(8,128)(2,1)} %param.35) | copy-start | bytes 786436
  9.2 35.4 %copy-start.16 = (bf16[64,2048]{1,0:T(8,128)(2,1)S(1)}, bf16[64,2048]{1,0:T(8,128)(2,1)}, u32[]{:S(2)}) copy-start(bf16[64,2048]{1,0:T(8,128)(2,1)} %param.29) | copy-start | bytes 786436
  42.8 1.8 copy-start.1
  46.1 16.3 %copy-start.14 = (pred[128]{0:T(512)(128)(4,1)S(1)}, pred[128]{0:T(512)(128)(4,1)}, u32[]{:S(2)}) copy-start(pred[128]{0:T(512)(128)(4,1)} %constant.8.clone.1) | copy-start | bytes 388
  60.2 5.2 %copy-start.12 = (bf16[3584,64]{0,1:T(8,128)(2,1)S(1)}, bf16[3584,64]{0,1:T(8,128)(2,1)}, u32[]{:S(2)}) copy-start(bf16[3584,64]{0,1:T(8,128)(2,1)} %param.28) | copy-start | bytes 1376260
  65.9 3.0 %copy-start.8 = (bf16[64,3584]{1,0:T(8,128)(2,1)S(1)}, bf16[64,3584]{1,0:T(8,128)(2,1)}, u32[]{:S(2)}) copy-start(bf16[64,3584]{1,0:T(8,128)(2,1)} %param.31) | copy-start | bytes 1376260
  67.4 1.5 copy-start.9
  67.4 2.4 %copy-start.10 = (bf16[64,3584]{1,0:T(8,128)(2,1)S(1)}, bf16[64,3584]{1,0:T(8,128)(2,1)}, u32[]{:S(2)}) copy-start(bf16[64,3584]{1,0:T(8,128)(2,1)} %param.33) | copy-start | bytes 1376260
  67.4 2.4 %copy-start.11 = (bf16[64,3584]{1,0:T(8,128)(2,1)S(1)}, bf16[64,3584]{1,0:T(8,128)(2,1)}, u32[]{:S(2)}) copy-start(bf16[64,3584]{1,0:T(8,128)(2,1)} %param.27) | copy-start | bytes 1376260
  176.9 1.7 copy-start.13
  176.9 27.7 %copy-start.2 = (bf16[8,32,2048]{2,1,0:T(8,128)(2,1)S(1)}, bf16[8,32,2048]{2,1,0:T(8,128)(2,1)}, u32[]{:S(2)}) copy-start(bf16[8,32,2048]{2,1,0:T(8,128)(2,1)} %get-tuple-element.18) | copy-start | bytes 3145732
  179.2 27.4 %copy-start = (bf16[8,32,2048]{2,1,0:T(8,128)(2,1)S(1)}, bf16[8,32,2048]{2,1,0:T(8,128)(2,1)}, u32[]{:S(2)}) copy-start(bf16[8,32,2048]{2,1,0:T(8,128)(2,1)} %get-tuple-element.17) | copy-start | bytes 3145732
  206.6 12.4 %copy-start.3 = (bf16[2048,64]{0,1:T(8,128)(2,1)S(1)}, bf16[2048,64]{0,1:T(8,128)(2,1)}, u32[]{:S(2)}) copy-start(bf16[2048,64]{0,1:T(8,128)(2,1)} %param.24) | copy-start | bytes 786436
  206.6 12.4 %copy-start.4 = (bf16[2048,64]{0,1:T(8,128)(2,1)S(1)}, bf16[2048,64]{0,1:T(8,128)(2,1)}, u32[]{:S(2)}) copy-start(bf16[2048,64]{0,1:T(8,128)(2,1)} %param.26) | copy-start | bytes 786436
  210.7 10.3 %copy-start.7 = (f32[64,3584]{1,0:T(8,128)S(1)}, f32[64,3584]{1,0:T(8,128)}, u32[]{:S(2)}) copy-start(f32[64,3584]{1,0:T(8,128)} %get-tuple-element.47) | copy-start | bytes 2752516
  220.0 1.9 copy-start.6
  221.0 1.9 copy-start.5
Sparse Core Ops, SparseCore 0:
  177.1 40.9 reduce-scatter.1
where the time goes:
time: 231 us
  Pallas kernels  171 us (74%)
  local copies, waits for them, and re-layouts  17.4 us (8%)
  between operations  14.4 us (6%)
  other arithmetic  10.3 us (4%)
  matrix products  10.2 us (4%)
  waiting for transfers between devices  7.36 us (3%)
    pallas_call x1, Pallas kernels, fused_block(): pl.pallas_call(block_kernel, out_shape=[jax.ShapeDtypeStruct((2 * count,...  106 us
    pallas_call x2, Pallas kernels, shard_total(): pl.pallas_call(functools.partial(total_kernel, axis, n), out_shape=jax.Sh...  33.3 us
    pallas_call x1, Pallas kernels, gathered(): pl.pallas_call(gather_kernel, out_shape=[jax.ShapeDtypeStruct(whole, jnp....  31.6 us
    unnamed x49, local copies, waits for them, and re-layouts  8.38 us
    reduce_scatter x1, waiting for transfers between devices, on_device(): lax.psum_scatter(feature.astype(jnp.bfloat16).reshape(2, count, width_row...  7.34 us
    dot_general x3, matrix products, summed_over_rows(): lax.dot_general(left, right, (((0,), (0,)), ((), ())), preferred_element_...  6.02 us
  transfers between devices with their start and end apart: 1, of which 1 were waited for; matrix products, arithmetic and copies ran while one was open for 6% of the time, Pallas kernels for 9%

commit v1 on v0

v1 whole, which is shorter than its diff:
```python
import functools

import jax
import jax.numpy as jnp
from jax import lax
from jax.experimental import pallas as pl
from jax.experimental.pallas import tpu as pltpu
from jax.sharding import PartitionSpec as P

adapter_scale = 0.5
epsilon = 1e-05
MESH = pl.DeviceIdType.MESH


def total_kernel(axis, n, x_ref, o_ref, inbox, whole, send1, recv1, send2, recv2):
    me = lax.axis_index(axis)
    barrier = pltpu.get_barrier_semaphore()

    @pl.loop(1, n)
    def _(k):
        pl.semaphore_signal(
            barrier, inc=1, device_id={axis: lax.rem(me + k, n)}, device_id_type=MESH
        )

    pl.semaphore_wait(barrier, n - 1)

    def scatter(k):
        peer = lax.rem(me + k, n)
        return pltpu.make_async_remote_copy(
            src_ref=x_ref.at[peer],
            dst_ref=inbox.at[k],
            send_sem=send1.at[k],
            recv_sem=recv1.at[k],
            device_id={axis: peer},
            device_id_type=MESH,
        )

    def spread(k):
        peer = lax.rem(me + k, n)
        return pltpu.make_async_remote_copy(
            src_ref=whole.at[me],
            dst_ref=whole.at[me],
            send_sem=send2.at[k],
            recv_sem=recv2.at[k],
            device_id={axis: peer},
            device_id_type=MESH,
        )

    def arrival(k):
        origin = lax.rem(me - k + n, n)
        return pltpu.make_async_remote_copy(
            src_ref=whole.at[origin],
            dst_ref=whole.at[origin],
            send_sem=send2.at[k],
            recv_sem=recv2.at[k],
            device_id={axis: origin},
            device_id_type=MESH,
        )

    @pl.loop(1, n)
    def _(k):
        scatter(k).start()

    def add(k, total):
        scatter(k).wait_recv()
        return total + inbox[k].astype(jnp.float32)

    total = lax.fori_loop(1, n, add, x_ref[me].astype(jnp.float32))
    whole[me] = total.astype(whole.dtype)

    @pl.loop(1, n)
    def _(k):
        spread(k).start()

    @pl.loop(1, n)
    def _(k):
        arrival(k).wait_recv()

    @pl.loop(1, n)
    def _(k):
        scatter(k).wait_send()
        spread(k).wait_send()

    o_ref[...] = whole[...]


def shard_total(x, axis, collective_id):
    n = lax.axis_size(axis)
    rows, columns = x.shape
    block = (n, rows // n, columns)
    total = pl.pallas_call(
        functools.partial(total_kernel, axis, n),
        out_shape=jax.ShapeDtypeStruct(block, jnp.bfloat16),
        in_specs=[pl.BlockSpec(memory_space=pltpu.VMEM)],
        out_specs=pl.BlockSpec(memory_space=pltpu.VMEM),
        scratch_shapes=[
            pltpu.VMEM(block, x.dtype),
            pltpu.VMEM(block, jnp.bfloat16),
            pltpu.SemaphoreType.DMA((n,)),
            pltpu.SemaphoreType.DMA((n,)),
            pltpu.SemaphoreType.DMA((n,)),
            pltpu.SemaphoreType.DMA((n,)),
        ],
        compiler_params=pltpu.CompilerParams(collective_id=collective_id, has_side_effects=True),
        name=f"total_{axis}",
    )(x.reshape(block))
    return total.reshape(rows, columns)


def curvature_product(left, right):
    return jnp.dot(left, right, preferred_element_type=jnp.float32)


def cross_shard_total(left, right):
    return lax.dot_general(
        left, right, (((1,), (1,)), ((), ())), preferred_element_type=jnp.float32
    )


def summed_over_rows(left, right):
    return lax.dot_general(
        left, right, (((0,), (0,)), ((), ())), preferred_element_type=jnp.float32
    )


def second_order(
    gate_preactivation,
    up_preactivation,
    hidden_adjoint,
    gate_tangent_rows,
    up_tangent_rows,
    adjoint_tangent_rows,
):
    sigma = jax.nn.sigmoid(gate_preactivation)
    silu_value = gate_preactivation * sigma
    slope = sigma * (1.0 + gate_preactivation * (1.0 - sigma))
    bend = sigma * (1.0 - sigma) * (2.0 + gate_preactivation * (1.0 - 2.0 * sigma))
    hidden_activation = (silu_value * up_preactivation).astype(jnp.bfloat16)
    hidden_direction = (
        slope * gate_tangent_rows * up_preactivation + silu_value * up_tangent_rows
    ).astype(jnp.bfloat16)
    gate_derivative = (hidden_adjoint * up_preactivation * slope).astype(jnp.bfloat16)
    up_derivative = (hidden_adjoint * silu_value).astype(jnp.bfloat16)
    gate_derivative_direction = (
        adjoint_tangent_rows * up_preactivation * slope
        + hidden_adjoint * (up_tangent_rows * slope + up_preactivation * bend * gate_tangent_rows)
    ).astype(jnp.bfloat16)
    up_derivative_direction = (
        adjoint_tangent_rows * silu_value + hidden_adjoint * slope * gate_tangent_rows
    ).astype(jnp.bfloat16)
    return (
        hidden_activation,
        hidden_direction,
        gate_derivative,
        up_derivative,
        gate_derivative_direction,
        up_derivative_direction,
    )


def lora_kernel(
    lead,
    tokens,
    gain,
    cot,
    gate_hbm,
    up_hbm,
    down_hbm,
    gate_in,
    gate_in_dir,
    up_in,
    up_in_dir,
    down_b,
    down_b_dir,
    gate_out,
    gate_out_dir,
    up_out,
    up_out_dir,
    down_in,
    down_in_dir,
    primal_ref,
    dir_ref,
    gate_curve_in,
    gate_curve,
    up_curve_in,
    up_curve,
    down_curve,
    down_curve_out,
    x_buf,
    cot_buf,
    squares,
    rank_part,
    rank_in,
    rank_all,
    in_rows,
    out_rows,
    wide_buf,
    down_buf,
    own_parts,
    own_first,
    own_mid_out,
    own_mid_in,
    own_whole,
    rest_parts,
    rest_first,
    rest_mid_out,
    rest_mid_in,
    rest_whole,
    own_left,
    own_flip,
    rest_left,
    rest_flip,
    total,
    gate_q,
    up_q,
    low_q,
    pair_out,
    pair_in,
    pair_q_out,
    pair_q_in,
    line_out,
    line_in,
    line_q_out,
    line_q_in,
    last_out,
    last_in,
    last_q_out,
    last_q_in,
    q_all,
    factor_sem,
    wide_sem,
    down_sem,
    square_sem,
    rank_sem,
    far_send,
    far_recv,
    near_send,
    near_recv,
    rank_all_sem,
    own_send,
    own_recv,
    rest_send,
    rest_recv,
    pair_sem,
    line_sem,
    last_sem,
    q_sem,
):
    row, me = lax.axis_index("row"), lax.axis_index("col")
    rows, columns = 4, 8
    z, core = me // 2, lax.rem(me, 2)
    partner = me + 1 - 2 * core
    flip_low = row + 1 - 2 * lax.rem(row, 2)
    flip_high = row + 2 - 4 * (row // 2)
    flip_both = 3 - row
    own, depth = tokens.shape
    chip = 2 * own
    count = 8 * own
    chunks = own_parts.shape[0]
    width = down_buf.shape[1]
    half = width // 2
    rank = gate_in.shape[0]
    slots, sides = wide_buf.shape[0], down_buf.shape[0]
    steps = 2 * chunks
    big = 4 * steps
    f32, bf16 = jnp.float32, jnp.bfloat16

    def remote(src, dst, send, recv, where):
        return pltpu.make_async_remote_copy(
            src_ref=src,
            dst_ref=dst,
            send_sem=send,
            recv_sem=recv,
            device_id=where,
            device_id_type=MESH,
        )

    def slot_rows(slot):
        return pl.ds(pl.multiple_of(slot * own, own), own)

    def lanes(c):
        return pl.ds(pl.multiple_of(c * width, width), width)

    def chunk_at(s):
        return (
            s - lead * ((s + big - lead) // big) - (chunks - lead) * ((s + big - lead - chunks) // big)
        )

    def loads(s):
        c, slot, side = chunk_at(s), lax.rem(s, slots), lax.rem(s, sides)
        return [
            pltpu.make_async_copy(
                gate_hbm.at[:, lanes(c)], wide_buf.at[slot, 0], wide_sem.at[slot, 0]
            ),
            pltpu.make_async_copy(
                up_hbm.at[:, lanes(c)], wide_buf.at[slot, 1], wide_sem.at[slot, 1]
            ),
            pltpu.make_async_copy(down_hbm.at[lanes(c), :], down_buf.at[side], down_sem.at[side]),
        ]

    factor_loads = []
    for index, (src, dst) in enumerate(
        [
            (down_b, in_rows.at[2, 0:rank]),
            (down_b_dir, in_rows.at[2, rank : 2 * rank]),
            (gate_in, in_rows.at[0, 0:rank]),
            (gate_in_dir, in_rows.at[0, rank : 2 * rank]),
            (up_in, in_rows.at[1, 0:rank]),
            (up_in_dir, in_rows.at[1, rank : 2 * rank]),
            (gate_out, out_rows.at[0, 0:rank]),
            (gate_out_dir, out_rows.at[0, rank : 2 * rank]),
            (up_out, out_rows.at[1, 0:rank]),
            (up_out_dir, out_rows.at[1, rank : 2 * rank]),
            (down_in, out_rows.at[2, 0:rank]),
            (down_in_dir, out_rows.at[2, rank : 2 * rank]),
        ]
    ):
        factor_loads.append(pltpu.make_async_copy(src, dst, factor_sem.at[index]))

    for copy in factor_loads[:6]:
        copy.start()
    for s in range(2):
        for copy in loads(s):
            copy.start()
    for copy in factor_loads[6:]:
        copy.start()

    line_in[...] = jnp.zeros_like(line_in)
    line_q_in[...] = jnp.zeros_like(line_q_in)

    barrier = pltpu.get_barrier_semaphore()

    def row_peer(k):
        return {"row": lax.rem(row + k, rows)}

    def col_peer(k):
        return {"col": lax.rem(me + k, columns)}

    @pl.loop(1, rows)
    def _(k):
        pl.semaphore_signal(barrier, inc=1, device_id=row_peer(k), device_id_type=MESH)

    @pl.loop(1, columns)
    def _(k):
        pl.semaphore_signal(barrier, inc=1, device_id=col_peer(k), device_id_type=MESH)

    values = tokens[...].astype(f32)
    squares[0] = jnp.broadcast_to(
        jnp.sum(values * values, axis=1, keepdims=True), squares.shape[1:]
    )
    cot_buf[slot_rows(core), :] = cot[...]
    pl.semaphore_wait(barrier, rows + columns - 2)

    def square(k):
        return remote(
            squares.at[0], squares.at[k], square_sem.at[0, k], square_sem.at[1, k], row_peer(k)
        )

    buffers = (cot_buf, x_buf)
    right, left = {"col": me + 2}, {"col": me - 2}

    def far(which, side, k):
        buffer = buffers[which]
        src = 2 * lax.rem(4 - k, 4) + core if side == 0 else 2 * k + core
        dst = 2 * (3 - k) + core if side == 0 else 2 * (k + 1) + core
        landing = 3 - k if side == 0 else k + 1
        return remote(
            buffer.at[slot_rows(src)],
            buffer.at[slot_rows(dst)],
            far_send.at[which, side, k],
            far_recv.at[which, landing],
            right if side == 0 else left,
        )

    def far_valid(side, k):
        if side == 0:
            return (z < 3) & (z >= k)
        return (z > 0) & (z + k <= 3)

    def far_arrival(which, slot):
        buffer = buffers[which]
        at = buffer.at[slot_rows(2 * slot + core)]
        return remote(at, at, far_send.at[which, 0, 0], far_recv.at[which, slot], {"col": partner})

    def near(which, slot):
        buffer = buffers[which]
        at = buffer.at[slot_rows(2 * slot + core)]
        return remote(
            at, at, near_send.at[which, slot], near_recv.at[which, slot], {"col": partner}
        )

    def near_arrival(which, slot):
        buffer = buffers[which]
        at = buffer.at[slot_rows(2 * slot + 1 - core)]
        return remote(
            at, at, near_send.at[which, slot], near_recv.at[which, slot], {"col": partner}
        )

    def launch(which):
        for side in range(2):

            @pl.when(far_valid(side, 0))
            def _(side=side):
                far(which, side, 0).start()

        near(which, 0).start()

    def pass_on(which, k):
        @pl.when(z >= k)
        def _():
            far_arrival(which, 4 - k).wait_recv()
            if k < 3:

                @pl.when(far_valid(0, k))
                def _():
                    far(which, 0, k).start()

            near(which, 4 - k).start()

        @pl.when(z + k <= 3)
        def _():
            far_arrival(which, k).wait_recv()
            if k < 3:

                @pl.when(far_valid(1, k))
                def _():
                    far(which, 1, k).start()

            near(which, k).start()

    for k in range(1, rows):
        square(k).start()
    launch(0)
    for copy in factor_loads[:6]:
        copy.wait()
    rank_part[:, 4 * rank :] = cross_shard_total(cot[...], in_rows[2]).astype(bf16)
    sum_squares = squares[0]
    for k in range(1, rows):
        square(k).wait_recv()
        sum_squares = sum_squares + squares[k]
    scale = lax.rsqrt(sum_squares[:, :1] / (rows * depth) + epsilon)
    x_buf[slot_rows(core), :] = (tokens[...].astype(f32) * scale * gain[...]).astype(bf16)
    launch(1)
    own_x = x_buf[slot_rows(core), :]
    rank_part[:, : 2 * rank] = cross_shard_total(own_x, in_rows[0]).astype(bf16)
    rank_part[:, 2 * rank : 4 * rank] = cross_shard_total(own_x, in_rows[1]).astype(bf16)

    def rank_row(k):
        return remote(
            rank_part, rank_in.at[k], rank_sem.at[0, k], rank_sem.at[1, k], row_peer(k)
        )

    for k in range(1, rows):
        rank_row(k).start()

    total[...] = jnp.zeros_like(total)
    for ref in (gate_q, up_q, low_q, gate_curve, up_curve, down_curve):
        ref[...] = jnp.zeros_like(ref)

    def slot_there(k):
        there = lax.rem(me + k, columns) // 2
        return 2 * lax.rem(z - there + 4, 4) + core

    def slot_from(k):
        origin = lax.rem(me - k + columns, columns)
        return 2 * lax.rem(origin // 2 - z + 4, 4) + lax.rem(origin, 2)

    def spread(buffer, sem, k):
        return remote(
            buffer.at[slot_rows(core)],
            buffer.at[slot_rows(slot_there(k))],
            sem.at[0, k],
            sem.at[1, k],
            col_peer(k),
        )

    def spread_arrival(buffer, sem, k):
        at = buffer.at[slot_rows(slot_from(k))]
        return remote(at, at, sem.at[0, k], sem.at[1, k], col_peer(k))

    def share_ranks():
        summed = rank_part[...].astype(f32)
        for k in range(1, rows):
            rank_row(k).wait_recv()
            summed = summed + rank_in[k].astype(f32)
        rank_all[slot_rows(core), :] = summed.astype(bf16)

        @pl.loop(1, columns)
        def _(k):
            spread(rank_all, rank_all_sem, k).start()

    partner_step = 7 - 6 * core

    class Group:
        pass

    mine, others = Group(), Group()
    mine.first, mine.size = 0, chip
    mine.parts, mine.inbox, mine.mid_out, mine.mid_in, mine.whole = (
        own_parts,
        own_first,
        own_mid_out,
        own_mid_in,
        own_whole,
    )
    mine.left, mine.flip, mine.send, mine.recv = own_left, own_flip, own_send, own_recv
    others.first, others.size = chip, count - chip
    others.parts, others.inbox, others.mid_out, others.mid_in, others.whole = (
        rest_parts,
        rest_first,
        rest_mid_out,
        rest_mid_in,
        rest_whole,
    )
    others.left, others.flip, others.send, others.recv = (
        rest_left,
        rest_flip,
        rest_send,
        rest_recv,
    )

    def prepare(g):
        low = rank_all[g.first : g.first + g.size, :].astype(f32)
        for index in range(3):
            block = low[:, index * 2 * rank : (index + 1) * 2 * rank] * adapter_scale
            lane = lax.broadcasted_iota(jnp.int32, block.shape, 1)
            turned = pltpu.roll(block, rank, 1)
            g.left[index, 0 : g.size, :] = jnp.where(lane < rank, block, 0.0).astype(bf16)
            g.left[index, g.size :, :] = turned.astype(bf16)
            g.flip[index] = turned.T.astype(bf16)

    def ends(path):
        return (flip_low, flip_high) if path == 0 else (flip_high, flip_low)

    def send(g, src, dst, c, path, k, peer):
        return remote(src, dst, g.send.at[c, path, k], g.recv.at[c, path, k], {"row": peer})

    def sends(g, c, path, ks):
        near_end, far_end = ends(path)
        table = [
            (g.parts.at[c, path, near_end], g.inbox.at[c, path, 0], near_end),
            (g.parts.at[c, path, flip_both], g.inbox.at[c, path, 1], near_end),
            (g.mid_out.at[c, path], g.mid_in.at[c, path], far_end),
            (g.whole.at[c, path, row], g.whole.at[c, path, row], far_end),
            (g.whole.at[c, path, row], g.whole.at[c, path, row], near_end),
            (g.whole.at[c, path, far_end], g.whole.at[c, path, far_end], near_end),
        ]
        return [send(g, table[k][0], table[k][1], c, path, k, table[k][2]) for k in ks]

    def arrivals(g, c, path, ks):
        near_end, far_end = ends(path)
        table = [
            (g.parts.at[c, path, row], g.inbox.at[c, path, 0], near_end),
            (g.parts.at[c, path, far_end], g.inbox.at[c, path, 1], near_end),
            (g.mid_out.at[c, path], g.mid_in.at[c, path], far_end),
            (g.whole.at[c, path, far_end], g.whole.at[c, path, far_end], far_end),
            (g.whole.at[c, path, near_end], g.whole.at[c, path, near_end], near_end),
            (g.whole.at[c, path, flip_both], g.whole.at[c, path, flip_both], near_end),
        ]
        return [send(g, table[k][0], table[k][1], c, path, k, table[k][2]) for k in ks]

    def project(g, c, s):
        for copy in loads(s):
            copy.wait()

        @pl.when(s + 2 < steps)
        def _():
            for copy in loads(s + 2):
                copy.start()

        slot = lax.rem(s, slots)
        span = slice(g.first, g.first + g.size)
        quarter = g.size // 4

        def put(path, at, value):
            g.parts[c, path, :, :, at : at + value.shape[1]] = value.reshape(
                4, quarter, value.shape[1]
            )

        gate = curvature_product(x_buf[span, :], wide_buf[slot, 0]).astype(bf16)
        put(0, 0, gate)
        up = curvature_product(x_buf[span, :], wide_buf[slot, 1]).astype(bf16)
        put(0, width, up[:, :half])
        put(1, 0, up[:, half:])
        for copy in sends(g, c, 0, (0, 1)):
            copy.start()
        down = cross_shard_total(cot_buf[span, :], down_buf[lax.rem(s, sides)]).astype(bf16)
        put(1, half, down)
        for copy in sends(g, c, 1, (0, 1)):
            copy.start()

    def relay(g, c, s):
        for path in range(2):
            near_end, far_end = ends(path)
            for copy in arrivals(g, c, path, (0, 1)):
                copy.wait_recv()
            g.mid_out[c, path] = (
                g.parts[c, path, far_end].astype(f32) + g.inbox[c, path, 1].astype(f32)
            ).astype(bf16)
            sends(g, c, path, (2,))[0].start()

    def settle(g, c, s):
        for path in range(2):
            arrivals(g, c, path, (2,))[0].wait_recv()
            g.whole[c, path, row] = (
                g.parts[c, path, row].astype(f32)
                + g.inbox[c, path, 0].astype(f32)
                + g.mid_in[c, path].astype(f32)
            ).astype(bf16)
            for copy in sends(g, c, path, (3, 4)):
                copy.start()

    def forward(g, c, s):
        for path in range(2):
            arrivals(g, c, path, (3,))[0].wait_recv()
            sends(g, c, path, (5,))[0].start()

    def differentiate(g, c, s):
        for path in range(2):
            for copy in arrivals(g, c, path, (4, 5)):
                copy.wait_recv()
        size = g.size

        def got(path, at, wide):
            return g.whole[c, path, :, :, at : at + wide].reshape(size, wide).astype(f32)

        gate_w, up_w, down_w = out_rows[0, :, lanes(c)], out_rows[1, :, lanes(c)], out_rows[2, :, lanes(c)]
        gate_low = curvature_product(g.left[0], gate_w)
        up_low = curvature_product(g.left[1], up_w)
        adj_low = curvature_product(g.left[2], down_w)
        hidden, hidden_dir, d_gate, d_up, d_gate_dir, d_up_dir = second_order(
            got(0, 0, width) + gate_low[:size],
            jnp.concatenate([got(0, width, half), got(1, 0, half)], axis=1) + up_low[:size],
            got(1, half, width) + adj_low[:size],
            gate_low[size:],
            up_low[size:],
            adj_low[size:],
        )
        gate_d = jnp.concatenate([d_gate, d_gate_dir], axis=0)
        up_d = jnp.concatenate([d_up, d_up_dir], axis=0)
        hidden_d = jnp.concatenate([hidden_dir, hidden], axis=0)
        span = slice(g.first, g.first + size)
        gate_curve[:, lanes(c)] += curvature_product(
            g.flip[0, :rank], d_gate
        ) + curvature_product(g.flip[0, rank:], d_gate_dir)
        up_curve[:, lanes(c)] += curvature_product(g.flip[1, :rank], d_up) + curvature_product(
            g.flip[1, rank:], d_up_dir
        )
        down_curve[:, lanes(c)] += curvature_product(
            g.flip[2, rank:], hidden_dir
        ) + curvature_product(g.flip[2, :rank], hidden)
        for ref, value, weight in (
            (gate_q, gate_d, gate_w),
            (up_q, up_d, up_w),
            (low_q, hidden_d, down_w),
        ):
            product = cross_shard_total(value, weight)
            ref[0, span, :] += product[:size]
            ref[1, span, :] += product[size:]
        slot = lax.rem(s, slots)
        piece = 512 if depth % 512 == 0 else depth
        for start in range(0, depth, piece):
            at = slice(start, start + piece)
            product = cross_shard_total(gate_d, wide_buf[slot, 0, at, :]) + cross_shard_total(
                up_d, wide_buf[slot, 1, at, :]
            )
            total[0, span, at] += product[:size]
            total[1, span, at] += product[size:]

    def q_rows(slot):
        at = slot_rows(slot)
        lane = lax.broadcasted_iota(jnp.int32, (own, 2 * rank), 1)
        low_half = lane < rank
        gate = gate_q[0, at, :] + jnp.where(low_half, 0.0, pltpu.roll(gate_q[1, at, :], rank, 1))
        up = up_q[0, at, :] + jnp.where(low_half, 0.0, pltpu.roll(up_q[1, at, :], rank, 1))
        low = jnp.where(low_half, low_q[0, at, :] + pltpu.roll(low_q[1, at, :], rank, 1), 0.0)
        return jnp.concatenate([gate, up, low], axis=1)

    def pair(src, dst, at):
        return remote(src, dst, pair_sem.at[0, at], pair_sem.at[1, at], {"col": partner})

    def pairs():
        return [pair(pair_out, pair_in, 0), pair(pair_q_out, pair_q_in, 1)]

    def exchange():
        for k in range(1, 4):
            slot = 2 * k + 1 - core
            for kind in range(2):
                pair_out[k - 1, kind] = total[kind, slot_rows(slot), :].astype(bf16)
            pair_q_out[k - 1] = q_rows(slot).astype(bf16)
        for copy in pairs():
            copy.start()

    def line(side, k, kind):
        out = k - 1 if side == 0 else 3 - k
        src, dst = (line_out, line_in) if kind == 0 else (line_q_out, line_q_in)
        return remote(
            src.at[out],
            dst.at[side, k - 1],
            line_sem.at[0, side, k - 1, kind],
            line_sem.at[1, side, k - 1, kind],
            right if side == 0 else left,
        )

    def line_arrival(side, k, kind):
        src, dst = (line_out, line_in) if kind == 0 else (line_q_out, line_q_in)
        return remote(
            src.at[0],
            dst.at[side, k],
            line_sem.at[0, side, k, kind],
            line_sem.at[1, side, k, kind],
            {"col": partner},
        )

    def line_valid(side, k):
        return z + k <= 3 if side == 0 else z - k >= 0

    def line_fed(side):
        return z >= 1 if side == 0 else z <= 2

    def line_stage(i):
        if i == 1:
            for copy in pairs():
                copy.wait_recv()
        k = 4 - i
        for side in range(2):

            @pl.when(line_valid(side, k))
            def _(side=side):
                if k < 3:

                    @pl.when(line_fed(side))
                    def _():
                        for kind in range(2):
                            line_arrival(side, k, kind).wait_recv()

                at = k if side == 0 else 4 - k
                slot = 2 * at + core
                for kind in range(2):
                    value = total[kind, slot_rows(slot), :] + pair_in[at - 1, kind].astype(f32)
                    if k < 3:
                        value = value + line_in[side, k, kind].astype(f32)
                    line_out[at - 1, kind] = value.astype(bf16)
                value = q_rows(slot) + pair_q_in[at - 1].astype(f32)
                if k < 3:
                    value = value + line_q_in[side, k].astype(f32)
                line_q_out[at - 1] = value.astype(bf16)
                for kind in range(2):
                    line(side, k, kind).start()

    def line_end():
        for side in range(2):

            @pl.when(line_fed(side))
            def _(side=side):
                for kind in range(2):
                    line_arrival(side, 0, kind).wait_recv()

    rest_end = lead + chunks + 3
    late = [exchange] + [functools.partial(line_stage, i) for i in (1, 2, 3)]
    stride = 2
    late_at = [rest_end] + [rest_end + 1 + stride * i for i in range(3)]
    relays = [(which, k) for k in (1, 2, 3) for which in (0, 1)]
    early = max(lead - 1, 0)

    for which in range(2):
        near_arrival(which, 0).wait_recv()

    def arrive():
        for which, k in relays[early:]:
            pass_on(which, k)
        for which in range(2):
            for k in range(1, 4):
                near_arrival(which, k).wait_recv()

    last_step = steps + 4

    @pl.loop(0, last_step)
    def _(t):
        @pl.when(t == lead)
        def _():
            arrive()

        for lag, stage in enumerate((project, relay, settle, forward, differentiate)):
            s = t - lag
            turn = lead + chunks
            if lag == 4:

                @pl.when(t == 4)
                def _():
                    for copy in factor_loads[6:]:
                        copy.wait()
                    spread_arrival(rank_all, rank_all_sem, partner_step).wait_recv()
                    prepare(mine)

                @pl.when(t == lead + 4)
                def _():
                    @pl.loop(1, columns)
                    def _(k):
                        @pl.when(k != partner_step)
                        def _():
                            spread_arrival(rank_all, rank_all_sem, k).wait_recv()

                    prepare(others)

            @pl.when(((s >= 0) & (s < lead)) | ((s >= turn) & (s < steps)))
            def _(s=s, stage=stage):
                stage(mine, chunk_at(s), s)

            @pl.when((s >= lead) & (s < turn))
            def _(s=s, stage=stage):
                stage(others, s - lead, s)

        @pl.when(t == 0)
        def _():
            share_ranks()

        for index, (which, k) in enumerate(relays[:early]):

            @pl.when(t == index)
            def _(which=which, k=k):
                pass_on(which, k)

        for at, action in zip(late_at, late):
            if at < last_step:

                @pl.when(t == at)
                def _(action=action):
                    action()

    for at, action in zip(late_at, late):
        if at >= last_step:
            action()

    def lasts():
        return [
            remote(last_out, last_in, last_sem.at[0, 0], last_sem.at[1, 0], {"col": partner}),
            remote(last_q_out, last_q_in, last_sem.at[0, 1], last_sem.at[1, 1], {"col": partner}),
        ]

    last_q_out[...] = q_rows(1 - core).astype(bf16)
    lasts()[1].start()
    for kind in range(2):
        last_out[kind] = total[kind, slot_rows(1 - core), :].astype(bf16)
    lasts()[0].start()
    line_end()
    lasts()[1].wait_recv()
    q_own = (
        q_rows(core)
        + last_q_in[...].astype(f32)
        + line_q_in[0, 0].astype(f32)
        + line_q_in[1, 0].astype(f32)
    )
    q_all[slot_rows(core), :] = q_own.astype(bf16)

    @pl.loop(1, columns)
    def _(k):
        spread(q_all, q_sem, k).start()

    lasts()[0].wait_recv()
    lane = lax.broadcasted_iota(jnp.int32, (own, 2 * rank), 1)
    feature = [
        total[kind, slot_rows(core), :]
        + last_in[kind].astype(f32)
        + line_in[0, 0, kind].astype(f32)
        + line_in[1, 0, kind].astype(f32)
        for kind in range(2)
    ]
    for index in range(2):
        block = q_own[:, index * 2 * rank : (index + 1) * 2 * rank] * adapter_scale
        straight = jnp.where(lane < rank, block, 0.0).astype(bf16)
        turned = pltpu.roll(block, rank, 1).astype(bf16)
        feature[0] = feature[0] + curvature_product(straight, in_rows[index])
        feature[1] = feature[1] + curvature_product(turned, in_rows[index])
    primal_ref[...] = feature[0]
    dir_ref[...] = feature[1]

    @pl.loop(1, columns)
    def _(k):
        spread_arrival(q_all, q_sem, k).wait_recv()

    every = q_all[...].astype(f32) * adapter_scale
    lane = lax.broadcasted_iota(jnp.int32, (count, 2 * rank), 1)
    both = jnp.where(
        lane < rank, pltpu.roll(every[:, : 2 * rank], rank, 1), every[:, 2 * rank : 4 * rank]
    )
    both_t = both.T.astype(bf16)
    low_t = every[:, 4 * rank :].T.astype(bf16)
    gate_curve_in[...] = curvature_product(both_t[:rank], x_buf[...])
    up_curve_in[...] = curvature_product(both_t[rank:], x_buf[...])
    down_curve_out[...] = curvature_product(low_t[:rank], cot_buf[...])

    for k in range(1, rows):
        square(k).wait_send()
        rank_row(k).wait_send()
    for which in range(2):
        for side in range(2):
            for k in range(3):

                @pl.when(far_valid(side, k))
                def _(which=which, side=side, k=k):
                    far(which, side, k).wait_send()

        for k in range(4):
            near(which, k).wait_send()

    @pl.loop(1, columns)
    def _(k):
        spread(rank_all, rank_all_sem, k).wait_send()
        spread(q_all, q_sem, k).wait_send()

    @pl.loop(0, chunks)
    def _(c):
        for g in (mine, others):
            for path in range(2):
                for copy in sends(g, c, path, range(6)):
                    copy.wait_send()

    for copy in pairs() + lasts():
        copy.wait_send()
    for side in range(2):
        for k in range(1, 4):

            @pl.when(line_valid(side, k))
            def _(side=side, k=k):
                for kind in range(2):
                    line(side, k, kind).wait_send()


def fused(
    tokens,
    norm_gain,
    cotangent,
    gate_frozen_weight,
    up_frozen_weight,
    down_frozen_weight,
    gate_input_factor,
    gate_output_factor,
    up_input_factor,
    up_output_factor,
    down_input_factor,
    down_b,
    gate_input_factor_direction,
    gate_output_factor_direction,
    up_input_factor_direction,
    up_output_factor_direction,
    down_input_factor_direction,
    down_b_dir,
    width,
):
    own, depth = tokens.shape
    hidden = gate_frozen_weight.shape[1]
    rank = gate_output_factor.shape[0]
    chunks = hidden // width
    chip, rest, count = 2 * own, 6 * own, 8 * own
    lead = (3 * chunks) // 7
    half_panel = 3 * width // 2
    f32, bf16 = jnp.float32, jnp.bfloat16
    vmem = pl.BlockSpec(memory_space=pltpu.VMEM)
    anywhere = pl.BlockSpec(memory_space=pl.ANY)

    def reduce_buffers(size):
        quarter = size // 4
        return [
            pltpu.VMEM((chunks, 2, 4, quarter, half_panel), bf16),
            pltpu.VMEM((chunks, 2, 2, quarter, half_panel), bf16),
            pltpu.VMEM((chunks, 2, quarter, half_panel), bf16),
            pltpu.VMEM((chunks, 2, quarter, half_panel), bf16),
            pltpu.VMEM((chunks, 2, 4, quarter, half_panel), bf16),
        ]

    dma = pltpu.SemaphoreType.DMA
    slots, sides = 7, 3
    results = pl.pallas_call(
        functools.partial(lora_kernel, lead),
        out_shape=[
            jax.ShapeDtypeStruct((own, depth), f32),
            jax.ShapeDtypeStruct((own, depth), f32),
            jax.ShapeDtypeStruct((rank, depth), f32),
            jax.ShapeDtypeStruct((rank, hidden), f32),
            jax.ShapeDtypeStruct((rank, depth), f32),
            jax.ShapeDtypeStruct((rank, hidden), f32),
            jax.ShapeDtypeStruct((rank, hidden), f32),
            jax.ShapeDtypeStruct((rank, depth), f32),
        ],
        in_specs=[vmem] * 3 + [anywhere] * 15,
        out_specs=[vmem] * 8,
        scratch_shapes=[
            pltpu.VMEM((count, depth), bf16),
            pltpu.VMEM((count, depth), bf16),
            pltpu.VMEM((4, own, 128), f32),
            pltpu.VMEM((own, 6 * rank), bf16),
            pltpu.VMEM((4, own, 6 * rank), bf16),
            pltpu.VMEM((count, 6 * rank), bf16),
            pltpu.VMEM((3, 2 * rank, depth), bf16),
            pltpu.VMEM((3, 2 * rank, hidden), bf16),
            pltpu.VMEM((slots, 2, depth, width), bf16),
            pltpu.VMEM((sides, width, depth), bf16),
        ]
        + reduce_buffers(chip)
        + reduce_buffers(rest)
        + [
            pltpu.VMEM((3, 2 * chip, 2 * rank), bf16),
            pltpu.VMEM((3, 2 * rank, chip), bf16),
            pltpu.VMEM((3, 2 * rest, 2 * rank), bf16),
            pltpu.VMEM((3, 2 * rank, rest), bf16),
            pltpu.VMEM((2, count, depth), f32),
            pltpu.VMEM((2, count, 2 * rank), f32),
            pltpu.VMEM((2, count, 2 * rank), f32),
            pltpu.VMEM((2, count, 2 * rank), f32),
            pltpu.VMEM((3, 2, own, depth), bf16),
            pltpu.VMEM((3, 2, own, depth), bf16),
            pltpu.VMEM((3, own, 6 * rank), bf16),
            pltpu.VMEM((3, own, 6 * rank), bf16),
            pltpu.VMEM((3, 2, own, depth), bf16),
            pltpu.VMEM((2, 3, 2, own, depth), bf16),
            pltpu.VMEM((3, own, 6 * rank), bf16),
            pltpu.VMEM((2, 3, own, 6 * rank), bf16),
            pltpu.VMEM((2, own, depth), bf16),
            pltpu.VMEM((2, own, depth), bf16),
            pltpu.VMEM((own, 6 * rank), bf16),
            pltpu.VMEM((own, 6 * rank), bf16),
            pltpu.VMEM((count, 6 * rank), bf16),
            dma((12,)),
            dma((slots, 2)),
            dma((sides,)),
            dma((2, 4)),
            dma((2, 4)),
            dma((2, 2, 3)),
            dma((2, 4)),
            dma((2, 4)),
            dma((2, 4)),
            dma((2, 8)),
            dma((chunks, 2, 6)),
            dma((chunks, 2, 6)),
            dma((chunks, 2, 6)),
            dma((chunks, 2, 6)),
            dma((2, 2)),
            dma((2, 2, 3, 2)),
            dma((2, 2)),
            dma((2, 8)),
        ],
        compiler_params=pltpu.CompilerParams(
            collective_id=2, has_side_effects=True, vmem_limit_bytes=63 * 1024 * 1024
        ),
        name="lora",
    )(
        tokens,
        norm_gain.reshape(1, depth),
        cotangent,
        gate_frozen_weight,
        up_frozen_weight,
        down_frozen_weight,
        gate_input_factor.T,
        gate_input_factor_direction.T,
        up_input_factor.T,
        up_input_factor_direction.T,
        down_b,
        down_b_dir,
        gate_output_factor,
        gate_output_factor_direction,
        up_output_factor,
        up_output_factor_direction,
        down_input_factor.T,
        down_input_factor_direction.T,
    )
    primal, direction, gate_input, gate_output, up_input, up_output, down_input, down_output = (
        results
    )
    return (
        primal,
        direction,
        gate_input.T,
        gate_output,
        up_input.T,
        up_output,
        down_input.T,
        down_output,
    )


def gather_kernel(
    tokens,
    gain,
    cot,
    x_all,
    cot_all,
    x_buf,
    cot_buf,
    squares,
    square_send,
    square_recv,
    far_send,
    far_recv,
    near_send,
    near_recv,
):
    rows, columns = lax.axis_size("row"), lax.axis_size("col")
    chips = columns // 2
    my_row, me = lax.axis_index("row"), lax.axis_index("col")
    partner = me + 1 - 2 * lax.rem(me, 2)
    features = rows * tokens.shape[1]
    barrier = pltpu.get_barrier_semaphore()

    def row_peer(k):
        return {"row": lax.rem(my_row + k, rows)}

    def far_peer(k):
        return {"col": lax.rem(me + 2 * k, columns)}

    @pl.loop(1, rows)
    def _(k):
        pl.semaphore_signal(barrier, inc=1, device_id=row_peer(k), device_id_type=MESH)

    @pl.loop(1, chips)
    def _(k):
        pl.semaphore_signal(barrier, inc=1, device_id=far_peer(k), device_id_type=MESH)

    pl.semaphore_signal(barrier, inc=1, device_id={"col": partner}, device_id_type=MESH)

    buffers = (cot_buf, x_buf)

    def origin(k):
        return lax.rem(me - 2 * k + columns, columns)

    def square(k):
        return pltpu.make_async_remote_copy(
            src_ref=squares.at[0],
            dst_ref=squares.at[k],
            send_sem=square_send.at[k],
            recv_sem=square_recv.at[k],
            device_id=row_peer(k),
            device_id_type=MESH,
        )

    def far(which, k, slot):
        return pltpu.make_async_remote_copy(
            src_ref=buffers[which].at[slot],
            dst_ref=buffers[which].at[slot],
            send_sem=far_send.at[which, k],
            recv_sem=far_recv.at[which, k],
            device_id=far_peer(k),
            device_id_type=MESH,
        )

    def near(which, k, slot):
        return pltpu.make_async_remote_copy(
            src_ref=buffers[which].at[slot],
            dst_ref=buffers[which].at[slot],
            send_sem=near_send.at[which, k],
            recv_sem=near_recv.at[which, k],
            device_id={"col": partner},
            device_id_type=MESH,
        )

    def launch(which):
        @pl.loop(1, chips)
        def _(k):
            far(which, k, me).start()

        near(which, 0, me).start()

    values = tokens[...].astype(jnp.float32)
    squares[0] = jnp.broadcast_to(
        jnp.sum(values * values, axis=1, keepdims=True), squares.shape[1:]
    )
    cot_buf[me] = cot[...]
    pl.semaphore_wait(barrier, rows + chips - 1)

    @pl.loop(1, rows)
    def _(k):
        square(k).start()

    launch(0)

    def add(k, total):
        square(k).wait_recv()
        return total + squares[k]

    total = lax.fori_loop(1, rows, add, squares[0])
    scale = lax.rsqrt(total[:, :1] / features + epsilon)
    x_buf[me] = (tokens[...].astype(jnp.float32) * scale * gain[...]).astype(jnp.bfloat16)
    launch(1)
    for which in range(2):

        @pl.loop(1, chips)
        def _(k, which=which):
            far(which, k, origin(k)).wait_recv()
            near(which, k, origin(k)).start()

    for which in range(2):

        @pl.loop(0, chips)
        def _(k, which=which):
            near(which, k, lax.rem(partner - 2 * k + columns, columns)).wait_recv()

    @pl.loop(1, rows)
    def _(k):
        square(k).wait_send()

    for which in range(2):

        @pl.loop(1, chips)
        def _(k, which=which):
            far(which, k, me).wait_send()

        @pl.loop(0, chips)
        def _(k, which=which):
            near(which, k, origin(k)).wait_send()

    cot_all[...] = cot_buf[...]
    x_all[...] = x_buf[...]


def gathered(tokens, gain, cot):
    rows, columns = lax.axis_size("row"), lax.axis_size("col")
    own, depth = tokens.shape
    whole = (columns, own, depth)
    vmem = pl.BlockSpec(memory_space=pltpu.VMEM)
    x, panel = pl.pallas_call(
        gather_kernel,
        out_shape=[jax.ShapeDtypeStruct(whole, jnp.bfloat16)] * 2,
        in_specs=[vmem] * 3,
        out_specs=[vmem] * 2,
        scratch_shapes=[
            pltpu.VMEM(whole, jnp.bfloat16),
            pltpu.VMEM(whole, jnp.bfloat16),
            pltpu.VMEM((rows, own, 128), jnp.float32),
            pltpu.SemaphoreType.DMA((rows,)),
            pltpu.SemaphoreType.DMA((rows,)),
            pltpu.SemaphoreType.DMA((2, columns // 2)),
            pltpu.SemaphoreType.DMA((2, columns // 2)),
            pltpu.SemaphoreType.DMA((2, columns // 2)),
            pltpu.SemaphoreType.DMA((2, columns // 2)),
        ],
        compiler_params=pltpu.CompilerParams(collective_id=3, has_side_effects=True),
        name="gather",
    )(tokens, gain.reshape(1, depth), cot)
    return x.reshape(columns * own, depth), panel.reshape(columns * own, depth)


def chunk_count(width):
    for count in (4, 2):
        if width % (128 * count) == 0:
            return count
    return 1


def on_device(
    tokens,
    norm_gain,
    cotangent,
    gate_frozen_weight,
    up_frozen_weight,
    down_frozen_weight,
    gate_input_factor,
    gate_output_factor,
    up_input_factor,
    up_output_factor,
    down_input_factor,
    down_b,
    gate_input_factor_direction,
    gate_output_factor_direction,
    up_input_factor_direction,
    up_output_factor_direction,
    down_input_factor_direction,
    down_b_dir,
):
    width = 256
    if (
        lax.axis_size("row") == 4
        and lax.axis_size("col") == 8
        and gate_frozen_weight.shape[1] % (7 * width) == 0
        and gate_frozen_weight.shape[0] % 128 == 0
        and gate_input_factor.shape[1] == 64
        and tokens.shape[0] % 32 == 0
    ):
        return fused(
            tokens,
            norm_gain,
            cotangent,
            gate_frozen_weight,
            up_frozen_weight,
            down_frozen_weight,
            gate_input_factor,
            gate_output_factor,
            up_input_factor,
            up_output_factor,
            down_input_factor,
            down_b,
            gate_input_factor_direction,
            gate_output_factor_direction,
            up_input_factor_direction,
            up_output_factor_direction,
            down_input_factor_direction,
            down_b_dir,
            width,
        )
    rank = gate_input_factor.shape[1]
    width_rows, width_columns = gate_frozen_weight.shape
    own_count = tokens.shape[0]
    normed_tokens, cot_panel = gathered(tokens, norm_gain, cotangent)
    count = normed_tokens.shape[0]
    in_factors = jnp.concatenate(
        [
            gate_input_factor,
            up_input_factor,
            gate_input_factor_direction,
            up_input_factor_direction,
        ],
        axis=1,
    )
    out_factors = jnp.concatenate([down_b, down_b_dir], axis=0)

    projected = jnp.concatenate(
        [curvature_product(normed_tokens, in_factors), cross_shard_total(cot_panel, out_factors)],
        axis=1,
    )
    ranks = shard_total(projected, "row", 0)
    gate_out = jnp.concatenate([gate_output_factor, gate_output_factor_direction], axis=0)
    up_out = jnp.concatenate([up_output_factor, up_output_factor_direction], axis=0)
    down_in = jnp.concatenate([down_input_factor, down_input_factor_direction], axis=1)

    chunks = chunk_count(width_columns)
    wide = width_columns // chunks
    spans = [slice(index * wide, (index + 1) * wide) for index in range(chunks)]

    summed_chunks = []
    for span in spans:
        partial = (
            curvature_product(normed_tokens, gate_frozen_weight[:, span]).astype(jnp.bfloat16),
            curvature_product(normed_tokens, up_frozen_weight[:, span]).astype(jnp.bfloat16),
            cross_shard_total(cot_panel, down_frozen_weight[span]).astype(jnp.bfloat16),
        )
        if summed_chunks:
            partial, summed_chunks[-1] = lax.optimization_barrier((partial, summed_chunks[-1]))
        summed_chunks.append(lax.psum(partial, "row"))

    gate_low, up_low, gate_low_dir, up_low_dir, adj_low, adj_low_dir = [
        ranks[:, index * rank : (index + 1) * rank] for index in range(6)
    ]
    gate_pair = jnp.concatenate([gate_low_dir, gate_low], axis=1)
    up_pair = jnp.concatenate([up_low_dir, up_low], axis=1)
    adj_pair = jnp.concatenate([adj_low_dir, adj_low], axis=1)
    gate_stack = jnp.concatenate([gate_low_dir, gate_low], axis=0)
    up_stack = jnp.concatenate([up_low_dir, up_low], axis=0)
    adj_stack = jnp.concatenate([adj_low, adj_low_dir], axis=0)
    feature = 0.0
    gate_q = 0.0
    up_q = 0.0
    low_dir = 0.0
    gate_output, up_output, down_input = [], [], []
    for span, total in zip(spans, summed_chunks):
        gate_sum, up_sum, adj_sum = [value.astype(jnp.float32) for value in total]
        gate_pre = gate_sum + adapter_scale * curvature_product(
            gate_low, gate_output_factor[:, span]
        )
        up_pre = up_sum + adapter_scale * curvature_product(
            up_low, up_output_factor[:, span]
        )
        hidden_adj = adj_sum + adapter_scale * cross_shard_total(
            adj_low, down_input_factor[span]
        )
        gate_tan = adapter_scale * curvature_product(gate_pair, gate_out[:, span])
        up_tan = adapter_scale * curvature_product(up_pair, up_out[:, span])
        adj_tan = adapter_scale * cross_shard_total(adj_pair, down_in[span])
        hidden, hidden_dir, d_gate, d_up, d_gate_dir, d_up_dir = second_order(
            gate_pre, up_pre, hidden_adj, gate_tan, up_tan, adj_tan
        )
        gate_d = jnp.concatenate([d_gate, d_gate_dir], axis=0)
        up_d = jnp.concatenate([d_up, d_up_dir], axis=0)
        hidden_d = jnp.concatenate([hidden_dir, hidden], axis=0)
        gate_output.append(adapter_scale * summed_over_rows(gate_stack, gate_d))
        up_output.append(adapter_scale * summed_over_rows(up_stack, up_d))
        down_input.append(adapter_scale * summed_over_rows(hidden_d, adj_stack))
        gate_q = gate_q + cross_shard_total(gate_d, gate_out[:, span])
        up_q = up_q + cross_shard_total(up_d, up_out[:, span])
        low_dir = (
            low_dir
            + curvature_product(hidden_dir, down_input_factor[span])
            + curvature_product(hidden, down_input_factor_direction[span])
        )
        feature = (
            feature
            + cross_shard_total(gate_d, gate_frozen_weight[:, span])
            + cross_shard_total(up_d, up_frozen_weight[:, span])
        )
    gate_output = jnp.concatenate(gate_output, axis=1)
    up_output = jnp.concatenate(up_output, axis=1)
    down_input = jnp.concatenate(down_input, axis=0)

    summed = lax.psum_scatter(
        feature.astype(jnp.bfloat16).reshape(2, count, width_rows),
        "col",
        scatter_dimension=1,
        tiled=True,
    ).astype(jnp.float32)
    adjoints = shard_total(
        jnp.concatenate(
            [
                gate_q[:count, :rank],
                up_q[:count, :rank],
                gate_q[count:, :rank] + gate_q[:count, rank:],
                up_q[count:, :rank] + up_q[:count, rank:],
                low_dir,
            ],
            axis=1,
        ).astype(jnp.bfloat16),
        "col",
        1,
    )
    piece = lax.dynamic_slice_in_dim(adjoints, lax.axis_index("col") * own_count, own_count, 0)
    normed_feature_adjoint = summed[0] + adapter_scale * cross_shard_total(
        piece[:, : 2 * rank], in_factors[:, : 2 * rank]
    )
    normed_feature_adjoint_direction = summed[1] + adapter_scale * cross_shard_total(
        jnp.concatenate([piece[:, 2 * rank : 4 * rank], piece[:, : 2 * rank]], axis=1), in_factors
    )
    gate_input = adapter_scale * summed_over_rows(
        normed_tokens, adjoints[:, 2 * rank : 3 * rank]
    )
    up_input = adapter_scale * summed_over_rows(normed_tokens, adjoints[:, 3 * rank : 4 * rank])
    down_output = adapter_scale * summed_over_rows(adjoints[:, 4 * rank :], cot_panel)
    return (
        normed_feature_adjoint,
        normed_feature_adjoint_direction,
        gate_input,
        gate_output,
        up_input,
        up_output,
        down_input,
        down_output,
    )


def solution(mesh):
    in_specs = (
        P("col", "row"),
        P("row"),
        P("col", "row"),
        P("row", "col"),
        P("row", "col"),
        P("col", "row"),
        P("row", None),
        P(None, "col"),
        P("row", None),
        P(None, "col"),
        P("col", None),
        P(None, "row"),
        P("row", None),
        P(None, "col"),
        P("row", None),
        P(None, "col"),
        P("col", None),
        P(None, "row"),
    )
    out_specs = (
        P("col", "row"),
        P("col", "row"),
        P("row", None),
        P(None, "col"),
        P("row", None),
        P(None, "col"),
        P("col", None),
        P(None, "row"),
    )
    return jax.shard_map(
        on_device, mesh=mesh, in_specs=in_specs, out_specs=out_specs, check_vma=False
    )
```

time: 231 us -> 170 us (0.74)
  Pallas kernels: 171 us -> 153 us
  between operations: 14.4 us -> 0.65 us
  other arithmetic: 10.3 us -> 0 us
  matrix products: 10.2 us -> 0 us
  waiting for transfers between devices: 7.36 us -> 0 us
    pallas_call x4 -> x1, Pallas kernels: 171 us -> 153 us  [fused(): pl.pallas_call(functools.partial(lora_kernel, lead), out_shape=[jax.Shape...]
    dot_general x7 -> x0, matrix products: 10.2 us -> none  [the longest x3 6.02 us: summed_over_rows(): lax.dot_general(left, right, (((0,), (0,)), ((), ())), preferred_element_...]
    reduce_scatter x1 -> x0, waiting for transfers between devices: 7.34 us -> none  [on_device(): lax.psum_scatter(feature.astype(jnp.bfloat16).reshape(2, count, width_row...]
    unnamed x49 -> x8, local copies, waits for them, and re-layouts: 8.38 us -> 15.5 us
    concatenate x6 -> x0, local copies, waits for them, and re-layouts: 5.87 us -> none  [the longest x3 2.28 us: left(): jnp.concatenate([jnp.concatenate([low, empty], axis=1), jnp.concatenate([...]
    concatenate x8 -> x0, other arithmetic: 3.54 us -> none  [the longest x1 1.43 us: on_device(): jnp.concatenate([down_input_factor, down_input_factor_direction], axis=1)]
    slice x4 -> x0, local copies, waits for them, and re-layouts: 3.12 us -> none  [the longest x1 1.64 us: on_device(): gate_q[:count, :rank]]
    another operation x2 -> x0, other arithmetic: 2.87 us -> none
  transfers between devices with their start and end apart: 1 -> 0, of which waited for: 1 -> 0; matrix products, arithmetic and copies ran while one was open for 6% -> 0% of each run, Pallas kernels for 9% -> 0%
where the time goes in v1:
time: 170 us; the launch traced here: 169 us
  Pallas kernels  153 us (90%)
  local copies, waits for them, and re-layouts  15.5 us (9%)
    pallas_call x1, Pallas kernels, fused(): pl.pallas_call(functools.partial(lora_kernel, lead), out_shape=[jax.Shape...  153 us
    unnamed x8, local copies, waits for them, and re-layouts  15.5 us

profile of v1, /device:TPU:0, one launch (start us, length us, event | category | flops | bytes accessed | tf_op | source)
XLA Modules:
  0.0 169.5 jit_solution(11097921006051368850)
XLA Ops:
  0.6 153.4 %lora.1 = (f32[32,2048]{1,0:T(8,128)}, f32[32,2048]{1,0:T(8,128)}, f32[64,2048]{1,0:T(8,128)}, f32[64,3584]{1,0:T(8,128)}, f32[64,2048]{1,0:T(8,128)}, /*index=5...) custom-call(bf16[32,2048]{1,0:T(8,128)(2,1)} %tokens.1, f32[1,2048]{1,0:T(1,128)} %bitcast.19, ...), custom_call_target="tpu_custom_call" | custom-call | tf_op jit(solution)/shard_map/lora/pallas_call | solution.py:974
  154.0 1.7 copy.34
  155.7 1.7 copy.35
  157.3 1.9 %copy.36 = f32[2048,64]{0,1:T(8,128)} copy(f32[2048,64]{0,1:T(8,128)} %bitcast.12) | data formatting | bytes 1048576
  159.2 2.2 %copy.37 = f32[64,3584]{1,0:T(8,128)} copy(f32[64,3584]{1,0:T(8,128)} %get-tuple-element.35) | data formatting | bytes 1835008
  161.4 1.9 %copy.38 = f32[2048,64]{0,1:T(8,128)} copy(f32[2048,64]{0,1:T(8,128)} %bitcast.11) | data formatting | bytes 1048576
  163.3 2.2 %copy.39 = f32[64,3584]{1,0:T(8,128)} copy(f32[64,3584]{1,0:T(8,128)} %get-tuple-element.37) | data formatting | bytes 1835008
  165.4 2.2 %copy.40 = f32[3584,64]{0,1:T(8,128)} copy(f32[3584,64]{0,1:T(8,128)} %bitcast.10) | data formatting | bytes 1835008
  167.6 1.9 %copy.41 = f32[64,2048]{1,0:T(8,128)} copy(f32[64,2048]{1,0:T(8,128)} %get-tuple-element.39) | data formatting | bytes 1048576

commit v2 on v1

--- a/solution.py
+++ b/solution.py
@@ -160,6 +160,7 @@
 
 def lora_kernel(
     lead,
+    gap,
     tokens,
     gain,
     cot,
@@ -178,6 +179,14 @@
     up_out_dir,
     down_in,
     down_in_dir,
+    primal_out,
+    dir_out,
+    gate_curve_in_out,
+    gate_curve_hbm,
+    up_curve_in_out,
+    up_curve_hbm,
+    down_curve_hbm,
+    down_curve_out_out,
     primal_ref,
     dir_ref,
     gate_curve_in,
@@ -192,14 +201,13 @@
     rank_part,
     rank_in,
     rank_all,
+    inv_all,
     in_rows,
     out_rows,
     wide_buf,
     down_buf,
     own_parts,
     own_first,
-    own_mid_out,
-    own_mid_in,
     own_whole,
     rest_parts,
     rest_first,
@@ -237,6 +245,7 @@
     near_send,
     near_recv,
     rank_all_sem,
+    inv_sem,
     own_send,
     own_recv,
     rest_send,
@@ -245,6 +254,7 @@
     line_sem,
     last_sem,
     q_sem,
+    out_sem,
 ):
     row, me = lax.axis_index("row"), lax.axis_index("col")
     rows, columns = 4, 8
@@ -298,6 +308,22 @@
             pltpu.make_async_copy(down_hbm.at[lanes(c), :], down_buf.at[side], down_sem.at[side]),
         ]
 
+    barrier = pltpu.get_barrier_semaphore()
+
+    def row_peer(k):
+        return {"row": lax.rem(row + k, rows)}
+
+    def col_peer(k):
+        return {"col": lax.rem(me + k, columns)}
+
+    @pl.loop(1, rows)
+    def _(k):
+        pl.semaphore_signal(barrier, inc=1, device_id=row_peer(k), device_id_type=MESH)
+
+    @pl.loop(1, columns)
+    def _(k):
+        pl.semaphore_signal(barrier, inc=1, device_id=col_peer(k), device_id_type=MESH)
+
     factor_loads = []
     for index, (src, dst) in enumerate(
         [
@@ -325,30 +351,14 @@
     for copy in factor_loads[6:]:
         copy.start()
 
-    line_in[...] = jnp.zeros_like(line_in)
-    line_q_in[...] = jnp.zeros_like(line_q_in)
-
-    barrier = pltpu.get_barrier_semaphore()
-
-    def row_peer(k):
-        return {"row": lax.rem(row + k, rows)}
-
-    def col_peer(k):
-        return {"col": lax.rem(me + k, columns)}
-
-    @pl.loop(1, rows)
-    def _(k):
-        pl.semaphore_signal(barrier, inc=1, device_id=row_peer(k), device_id_type=MESH)
-
-    @pl.loop(1, columns)
-    def _(k):
-        pl.semaphore_signal(barrier, inc=1, device_id=col_peer(k), device_id_type=MESH)
-
     values = tokens[...].astype(f32)
     squares[0] = jnp.broadcast_to(
         jnp.sum(values * values, axis=1, keepdims=True), squares.shape[1:]
     )
     cot_buf[slot_rows(core), :] = cot[...]
+    x_buf[slot_rows(core), :] = (values * gain[...]).astype(bf16)
+    line_in[...] = jnp.zeros_like(line_in)
+    line_q_in[...] = jnp.zeros_like(line_q_in)
     pl.semaphore_wait(barrier, rows + columns - 2)
 
     def square(k):
@@ -428,19 +438,13 @@
 
             near(which, k).start()
 
+    launch(0)
+    launch(1)
     for k in range(1, rows):
         square(k).start()
-    launch(0)
     for copy in factor_loads[:6]:
         copy.wait()
     rank_part[:, 4 * rank :] = cross_shard_total(cot[...], in_rows[2]).astype(bf16)
-    sum_squares = squares[0]
-    for k in range(1, rows):
-        square(k).wait_recv()
-        sum_squares = sum_squares + squares[k]
-    scale = lax.rsqrt(sum_squares[:, :1] / (rows * depth) + epsilon)
-    x_buf[slot_rows(core), :] = (tokens[...].astype(f32) * scale * gain[...]).astype(bf16)
-    launch(1)
     own_x = x_buf[slot_rows(core), :]
     rank_part[:, : 2 * rank] = cross_shard_total(own_x, in_rows[0]).astype(bf16)
     rank_part[:, 2 * rank : 4 * rank] = cross_shard_total(own_x, in_rows[1]).astype(bf16)
@@ -453,9 +457,12 @@
     for k in range(1, rows):
         rank_row(k).start()
 
-    total[...] = jnp.zeros_like(total)
-    for ref in (gate_q, up_q, low_q, gate_curve, up_curve, down_curve):
-        ref[...] = jnp.zeros_like(ref)
+    pass_on(0, 1)
+
+    def clear():
+        total[...] = jnp.zeros_like(total)
+        for ref in (gate_q, up_q, low_q, gate_curve, up_curve, down_curve):
+            ref[...] = jnp.zeros_like(ref)
 
     def slot_there(k):
         there = lax.rem(me + k, columns) // 2
@@ -479,15 +486,26 @@
         return remote(at, at, sem.at[0, k], sem.at[1, k], col_peer(k))
 
     def share_ranks():
+        sum_squares = squares[0]
         summed = rank_part[...].astype(f32)
         for k in range(1, rows):
+            square(k).wait_recv()
+            sum_squares = sum_squares + squares[k]
             rank_row(k).wait_recv()
             summed = summed + rank_in[k].astype(f32)
-        rank_all[slot_rows(core), :] = summed.astype(bf16)
+        inv = lax.rsqrt(sum_squares / (rows * depth) + epsilon)
+        inv_all[slot_rows(core), :] = inv
+        for index in range(3):
+            at = slice(index * 2 * rank, (index + 1) * 2 * rank)
+            block = summed[:, at]
+            if index < 2:
+                block = block * inv
+            rank_all[slot_rows(core), at] = block.astype(bf16)
 
         @pl.loop(1, columns)
         def _(k):
             spread(rank_all, rank_all_sem, k).start()
+            spread(inv_all, inv_sem, k).start()
 
     partner_step = 7 - 6 * core
 
@@ -496,28 +514,9 @@
 
     mine, others = Group(), Group()
     mine.first, mine.size = 0, chip
-    mine.parts, mine.inbox, mine.mid_out, mine.mid_in, mine.whole = (
-        own_parts,
-        own_first,
-        own_mid_out,
-        own_mid_in,
-        own_whole,
-    )
-    mine.left, mine.flip, mine.send, mine.recv = own_left, own_flip, own_send, own_recv
+    mine.left, mine.flip = own_left, own_flip
     others.first, others.size = chip, count - chip
-    others.parts, others.inbox, others.mid_out, others.mid_in, others.whole = (
-        rest_parts,
-        rest_first,
-        rest_mid_out,
-        rest_mid_in,
-        rest_whole,
-    )
-    others.left, others.flip, others.send, others.recv = (
-        rest_left,
-        rest_flip,
-        rest_send,
-        rest_recv,
-    )
+    others.left, others.flip = rest_left, rest_flip
 
     def prepare(g):
         low = rank_all[g.first : g.first + g.size, :].astype(f32)
@@ -529,35 +528,66 @@
             g.left[index, g.size :, :] = turned.astype(bf16)
             g.flip[index] = turned.T.astype(bf16)
 
+    friends = (flip_both, flip_low, flip_high)
+
+    def own_sends(c, stage):
+        return [
+            remote(
+                own_parts.at[c, peer] if stage == 0 else own_whole.at[c, row],
+                own_first.at[c, index] if stage == 0 else own_whole.at[c, row],
+                own_send.at[c, stage],
+                own_recv.at[c, stage],
+                {"row": peer},
+            )
+            for index, peer in enumerate(friends)
+        ]
+
+    def own_all(c, stage):
+        return remote(
+            own_first.at[c],
+            own_first.at[c],
+            own_send.at[c, stage],
+            own_recv.at[c, stage],
+            {"row": flip_both},
+        )
+
     def ends(path):
         return (flip_low, flip_high) if path == 0 else (flip_high, flip_low)
 
-    def send(g, src, dst, c, path, k, peer):
-        return remote(src, dst, g.send.at[c, path, k], g.recv.at[c, path, k], {"row": peer})
-
-    def sends(g, c, path, ks):
+    def send(src, dst, c, path, k, peer):
+        away = rest_send.at[c, 1 if k in (2, 5) else 0]
+        landed = rest_recv.at[c, 6] if k > 3 else rest_recv.at[c, 3 * path + max(k - 1, 0)]
+        return remote(src, dst, away, landed, {"row": peer})
+
+    def sends(c, path, ks):
         near_end, far_end = ends(path)
         table = [
-            (g.parts.at[c, path, near_end], g.inbox.at[c, path, 0], near_end),
-            (g.parts.at[c, path, flip_both], g.inbox.at[c, path, 1], near_end),
-            (g.mid_out.at[c, path], g.mid_in.at[c, path], far_end),
-            (g.whole.at[c, path, row], g.whole.at[c, path, row], far_end),
-            (g.whole.at[c, path, row], g.whole.at[c, path, row], near_end),
-            (g.whole.at[c, path, far_end], g.whole.at[c, path, far_end], near_end),
+            (rest_parts.at[c, path, near_end], rest_first.at[c, path, 0], near_end),
+            (rest_parts.at[c, path, flip_both], rest_first.at[c, path, 1], near_end),
+            (rest_mid_out.at[c, path], rest_mid_in.at[c, path], far_end),
+            (rest_whole.at[c, path, row], rest_whole.at[c, path, row], far_end),
+            (rest_whole.at[c, path, row], rest_whole.at[c, path, row], near_end),
+            (rest_whole.at[c, path, far_end], rest_whole.at[c, path, far_end], near_end),
         ]
-        return [send(g, table[k][0], table[k][1], c, path, k, table[k][2]) for k in ks]
-
-    def arrivals(g, c, path, ks):
-        near_end, far_end = ends(path)
-        table = [
-            (g.parts.at[c, path, row], g.inbox.at[c, path, 0], near_end),
-            (g.parts.at[c, path, far_end], g.inbox.at[c, path, 1], near_end),
-            (g.mid_out.at[c, path], g.mid_in.at[c, path], far_end),
-            (g.whole.at[c, path, far_end], g.whole.at[c, path, far_end], far_end),
-            (g.whole.at[c, path, near_end], g.whole.at[c, path, near_end], near_end),
-            (g.whole.at[c, path, flip_both], g.whole.at[c, path, flip_both], near_end),
-        ]
-        return [send(g, table[k][0], table[k][1], c, path, k, table[k][2]) for k in ks]
+        return [send(table[k][0], table[k][1], c, path, k, table[k][2]) for k in ks]
+
+    def landed_pair(c, path):
+        at = rest_first.at[c, path]
+        return remote(at, at, rest_send.at[c, 0], rest_recv.at[c, 3 * path], {"row": flip_low})
+
+    def landed_one(c, path, k):
+        at = rest_mid_in.at[c, path]
+        return remote(
+            at, at, rest_send.at[c, 0], rest_recv.at[c, 3 * path + k - 1], {"row": flip_low}
+        )
+
+    def landed_four(c):
+        at = rest_first.at[c]
+        return remote(at, at, rest_send.at[c, 1], rest_recv.at[c, 6], {"row": flip_low})
+
+    def sent_eight(c):
+        at = rest_parts.at[c]
+        return remote(at, at, rest_send.at[c, 0], rest_recv.at[c, 6], {"row": flip_low})
 
     def project(g, c, s):
         for copy in loads(s):
@@ -572,66 +602,89 @@
         span = slice(g.first, g.first + g.size)
         quarter = g.size // 4
 
-        def put(path, at, value):
-            g.parts[c, path, :, :, at : at + value.shape[1]] = value.reshape(
-                4, quarter, value.shape[1]
-            )
-
-        gate = curvature_product(x_buf[span, :], wide_buf[slot, 0]).astype(bf16)
-        put(0, 0, gate)
-        up = curvature_product(x_buf[span, :], wide_buf[slot, 1]).astype(bf16)
-        put(0, width, up[:, :half])
-        put(1, 0, up[:, half:])
-        for copy in sends(g, c, 0, (0, 1)):
+        def put(at, value):
+            for start in range(0, width, half):
+                piece = value[:, start : start + half].reshape(4, quarter, half)
+                lane = at * width + start
+                if g is mine:
+                    own_parts[c, :, :, lane : lane + half] = piece
+                else:
+                    path, lane = lane // (3 * half), lane % (3 * half)
+                    rest_parts[c, path, :, :, lane : lane + half] = piece
+
+        put(0, curvature_product(x_buf[span, :], wide_buf[slot, 0]).astype(bf16))
+        put(1, curvature_product(x_buf[span, :], wide_buf[slot, 1]).astype(bf16))
+        if g is others:
+            for copy in sends(c, 0, (0, 1)):
+                copy.start()
+        put(2, cross_shard_total(cot_buf[span, :], down_buf[lax.rem(s, sides)]).astype(bf16))
+        for copy in own_sends(c, 0) if g is mine else sends(c, 1, (0, 1)):
             copy.start()
-        down = cross_shard_total(cot_buf[span, :], down_buf[lax.rem(s, sides)]).astype(bf16)
-        put(1, half, down)
-        for copy in sends(g, c, 1, (0, 1)):
+
+    def reduce(g, c, s):
+        own_all(c, 0).wait_recv()
+        summed = own_parts[c, row].astype(f32)
+        for index in range(3):
+            summed = summed + own_first[c, index].astype(f32)
+        own_whole[c, row] = summed.astype(bf16)
+        for copy in own_sends(c, 1):
             copy.start()
 
     def relay(g, c, s):
         for path in range(2):
             near_end, far_end = ends(path)
-            for copy in arrivals(g, c, path, (0, 1)):
-                copy.wait_recv()
-            g.mid_out[c, path] = (
-                g.parts[c, path, far_end].astype(f32) + g.inbox[c, path, 1].astype(f32)
+            landed_pair(c, path).wait_recv()
+            rest_mid_out[c, path] = (
+                rest_parts[c, path, far_end].astype(f32) + rest_first[c, path, 1].astype(f32)
             ).astype(bf16)
-            sends(g, c, path, (2,))[0].start()
+            sends(c, path, (2,))[0].start()
 
     def settle(g, c, s):
         for path in range(2):
-            arrivals(g, c, path, (2,))[0].wait_recv()
-            g.whole[c, path, row] = (
-                g.parts[c, path, row].astype(f32)
-                + g.inbox[c, path, 0].astype(f32)
-                + g.mid_in[c, path].astype(f32)
+            landed_one(c, path, 2).wait_recv()
+            rest_whole[c, path, row] = (
+                rest_parts[c, path, row].astype(f32)
+                + rest_first[c, path, 0].astype(f32)
+                + rest_mid_in[c, path].astype(f32)
             ).astype(bf16)
-            for copy in sends(g, c, path, (3, 4)):
+            for copy in sends(c, path, (3, 4)):
                 copy.start()
 
     def forward(g, c, s):
         for path in range(2):
-            arrivals(g, c, path, (3,))[0].wait_recv()
-            sends(g, c, path, (5,))[0].start()
+            landed_one(c, path, 3).wait_recv()
+            sends(c, path, (5,))[0].start()
 
     def differentiate(g, c, s):
-        for path in range(2):
-            for copy in arrivals(g, c, path, (4, 5)):
-                copy.wait_recv()
+        if g is mine:
+            own_all(c, 1).wait_recv()
+        else:
+            landed_four(c).wait_recv()
         size = g.size
 
-        def got(path, at, wide):
-            return g.whole[c, path, :, :, at : at + wide].reshape(size, wide).astype(f32)
+        def got(at):
+            pieces = []
+            for start in range(0, width, half):
+                lane = at * width + start
+                if g is mine:
+                    piece = own_whole[c, :, :, lane : lane + half]
+                else:
+                    path, lane = lane // (3 * half), lane % (3 * half)
+                    piece = rest_whole[c, path, :, :, lane : lane + half]
+                piece = piece.reshape(size, half).astype(f32)
+                if at < 2:
+                    piece = piece * inv_all[g.first : g.first + size, :]
+                pieces.append(piece)
+            return jnp.concatenate(pieces, axis=1)
 
         gate_w, up_w, down_w = out_rows[0, :, lanes(c)], out_rows[1, :, lanes(c)], out_rows[2, :, lanes(c)]
         gate_low = curvature_product(g.left[0], gate_w)
         up_low = curvature_product(g.left[1], up_w)
         adj_low = curvature_product(g.left[2], down_w)
         hidden, hidden_dir, d_gate, d_up, d_gate_dir, d_up_dir = second_order(
-            got(0, 0, width) + gate_low[:size],
-            jnp.concatenate([got(0, width, half), got(1, 0, half)], axis=1) + up_low[:size],
-            got(1, half, width) + adj_low[:size],
+            got(0) + gate_low[:size],
+            got(1) + up_low[:size],
+            got(2) + adj_low[:size],
             gate_low[size:],
             up_low[size:],
             adj_low[size:],
@@ -693,20 +746,21 @@
 
     def line(side, k, kind):
         out = k - 1 if side == 0 else 3 - k
-        src, dst = (line_out, line_in) if kind == 0 else (line_q_out, line_q_in)
+        src = line_out.at[out, kind] if kind < 2 else line_q_out.at[out]
+        dst = line_in.at[side, k - 1, kind] if kind < 2 else line_q_in.at[side, k - 1]
         return remote(
-            src.at[out],
-            dst.at[side, k - 1],
+            src,
+            dst,
             line_sem.at[0, side, k - 1, kind],
             line_sem.at[1, side, k - 1, kind],
             right if side == 0 else left,
         )
 
     def line_arrival(side, k, kind):
-        src, dst = (line_out, line_in) if kind == 0 else (line_q_out, line_q_in)
+        at = line_in.at[side, k, kind] if kind < 2 else line_q_in.at[side, k]
         return remote(
-            src.at[0],
-            dst.at[side, k],
+            at,
+            at,
             line_sem.at[0, side, k, kind],
             line_sem.at[1, side, k, kind],
             {"col": partner},
@@ -718,53 +772,66 @@
     def line_fed(side):
         return z >= 1 if side == 0 else z <= 2
 
-    def line_stage(i):
-        if i == 1:
-            for copy in pairs():
-                copy.wait_recv()
-        k = 4 - i
-        for side in range(2):
-
-            @pl.when(line_valid(side, k))
-            def _(side=side):
+    def line_send(side, k, kinds):
+        at = k if side == 0 else 4 - k
+        slot = 2 * at + core
+        for kind in kinds:
+            if kind < 2:
+                value = total[kind, slot_rows(slot), :] + pair_in[at - 1, kind].astype(f32)
                 if k < 3:
-
-                    @pl.when(line_fed(side))
-                    def _():
-                        for kind in range(2):
-                            line_arrival(side, k, kind).wait_recv()
-
-                at = k if side == 0 else 4 - k
-                slot = 2 * at + core
-                for kind in range(2):
-                    value = total[kind, slot_rows(slot), :] + pair_in[at - 1, kind].astype(f32)
-                    if k < 3:
-                        value = value + line_in[side, k, kind].astype(f32)
-                    line_out[at - 1, kind] = value.astype(bf16)
+                    value = value + line_in[side, k, kind].astype(f32)
+                line_out[at - 1, kind] = value.astype(bf16)
+            else:
                 value = q_rows(slot) + pair_q_in[at - 1].astype(f32)
                 if k < 3:
                     value = value + line_q_in[side, k].astype(f32)
                 line_q_out[at - 1] = value.astype(bf16)
-                for kind in range(2):
-                    line(side, k, kind).start()
+            line(side, k, kind).start()
+
+    def line_open():
+        for copy in pairs():
+            copy.wait_recv()
+        for side in range(2):
+            for k in (3, 2, 1):
+
+                @pl.when(line_valid(side, k) & ((z == 0) if side == 0 else (z == 3)))
+                def _(side=side, k=k):
+                    line_send(side, k, (0, 1, 2))
+
+    def line_stage(k, kinds):
+        for side in range(2):
+
+            @pl.when(line_valid(side, k) & line_fed(side))
+            def _(side=side):
+                for kind in kinds:
+                    line_arrival(side, k, kind).wait_recv()
+                line_send(side, k, kinds)
 
     def line_end():
         for side in range(2):
 
             @pl.when(line_fed(side))
             def _(side=side):
-                for kind in range(2):
+                for kind in range(3):
                     line_arrival(side, 0, kind).wait_recv()
 
-    rest_end = lead + chunks + 3
-    late = [exchange] + [functools.partial(line_stage, i) for i in (1, 2, 3)]
-    stride = 2
-    late_at = [rest_end] + [rest_end + 1 + stride * i for i in range(3)]
-    relays = [(which, k) for k in (1, 2, 3) for which in (0, 1)]
-    early = max(lead - 1, 0)
-
-    for which in range(2):
-        near_arrival(which, 0).wait_recv()
+    turn = lead + chunks
+    resume = turn + gap
+    rest_end = turn + 3
+    late = {
+        rest_end: exchange,
+        rest_end + 1: line_open,
+        rest_end + 3: functools.partial(line_stage, 2, (0,)),
+        rest_end + 4: functools.partial(line_stage, 2, (1, 2)),
+        rest_end + 5: functools.partial(line_stage, 1, (0,)),
+        rest_end + 6: functools.partial(line_stage, 1, (1, 2)),
+    }
+    relays = [(1, 1), (0, 2), (1, 2), (0, 3), (1, 3)]
+    early = max(min(lead - 3, len(relays)), 0)
+
+    def share():
+        share_ranks()
+        clear()
 
     def arrive():
         for which, k in relays[early:]:
@@ -773,64 +840,82 @@
             for k in range(1, 4):
                 near_arrival(which, k).wait_recv()
 
-    last_step = steps + 4
+    def first_ready():
+        for copy in factor_loads[6:]:
+            copy.wait()
+        spread_arrival(rank_all, rank_all_sem, partner_step).wait_recv()
+        spread_arrival(inv_all, inv_sem, partner_step).wait_recv()
+        prepare(mine)
+
+    def rest_ready():
+        @pl.loop(1, columns)
+        def _(k):
+            @pl.when(k != partner_step)
+            def _():
+                spread_arrival(rank_all, rank_all_sem, k).wait_recv()
+                spread_arrival(inv_all, inv_sem, k).wait_recv()
+
+        prepare(others)
+
+    for which in range(2):
+        near_arrival(which, 0).wait_recv()
+
+    last_step = steps + gap + 4
 
     @pl.loop(0, last_step)
     def _(t):
-        @pl.when(t == lead)
-        def _():
-            arrive()
-
+        def at_step(step, action):
+            @pl.when(t == step)
+            def _():
+                action()
+
+        def own_stage(lag, stage):
+            u = t - lag
+            after = (u + big - resume) // big
+            s = u - gap * after
+
+            @pl.when(((u >= 0) & (u < lead)) | ((u >= resume) & (u < steps + gap)))
+            def _():
+                stage(mine, s - chunks * after, s)
+
+        def rest_stage(lag, stage):
+            s = t - lag
+
+            @pl.when((s >= lead) & (s < turn))
+            def _():
+                stage(others, s - lead, s)
+
+        at_step(lead, arrive)
+        at_step(4, first_ready)
+        at_step(lead + 4, rest_ready)
         for lag, stage in enumerate((project, relay, settle, forward, differentiate)):
-            s = t - lag
-            turn = lead + chunks
-            if lag == 4:
-
-                @pl.when(t == 4)
-                def _():
-                    for copy in factor_loads[6:]:
-                        copy.wait()
-                    spread_arrival(rank_all, rank_all_sem, partner_step).wait_recv()
-                    prepare(mine)
-
-                @pl.when(t == lead + 4)
-                def _():
-                    @pl.loop(1, columns)
-                    def _(k):
-                        @pl.when(k != partner_step)
-                        def _():
-                            spread_arrival(rank_all, rank_all_sem, k).wait_recv()
-
-                    prepare(others)
-
-            @pl.when(((s >= 0) & (s < lead)) | ((s >= turn) & (s < steps)))
-            def _(s=s, stage=stage):
-                stage(mine, chunk_at(s), s)
-
-            @pl.when((s >= lead) & (s < turn))
-            def _(s=s, stage=stage):
-                stage(others, s - lead, s)
-
-        @pl.when(t == 0)
-        def _():
-            share_ranks()
-
+            rest_stage(lag, stage)
+        for step, action in late.items():
+            if step < last_step:
+                at_step(step, action)
+        own_stage(0, project)
+        at_step(0, share)
+        own_stage(2, reduce)
+        own_stage(4, differentiate)
         for index, (which, k) in enumerate(relays[:early]):
-
-            @pl.when(t == index)
-            def _(which=which, k=k):
-                pass_on(which, k)
-
-        for at, action in zip(late_at, late):
-            if at < last_step:
-
-                @pl.when(t == at)
-                def _(action=action):
-                    action()
-
-    for at, action in zip(late_at, late):
-        if at >= last_step:
+            at_step(index + 1 + index // 3, functools.partial(pass_on, which, k))
+
+    for step, action in late.items():
+        if step >= last_step:
             action()
+
+    def outputs(index):
+        src, dst = (
+            (primal_ref, primal_out),
+            (dir_ref, dir_out),
+            (gate_curve_in, gate_curve_in_out),
+            (gate_curve, gate_curve_hbm),
+            (up_curve_in, up_curve_in_out),
+            (up_curve, up_curve_hbm),
+            (down_curve, down_curve_hbm),
+            (down_curve_out, down_curve_out_out),
+        )[index]
+        return pltpu.make_async_copy(src, dst, out_sem.at[index])
 
     def lasts():
         return [
@@ -838,13 +923,24 @@
             remote(last_q_out, last_q_in, last_sem.at[0, 1], last_sem.at[1, 1], {"col": partner}),
         ]
 
+    last_feature, last_q = lasts()
     last_q_out[...] = q_rows(1 - core).astype(bf16)
-    lasts()[1].start()
+    last_q.start()
     for kind in range(2):
         last_out[kind] = total[kind, slot_rows(1 - core), :].astype(bf16)
-    lasts()[0].start()
+    last_feature.start()
+    for index in (3, 5, 6):
+        outputs(index).start()
+
+    @pl.loop(0, chunks)
+    def _(c):
+        own_all(c, 0).wait_send()
+        own_all(c, 1).wait_send()
+        sent_eight(c).wait_send()
+        landed_four(c).wait_send()
+
     line_end()
-    lasts()[1].wait_recv()
+    last_q.wait_recv()
     q_own = (
         q_rows(core)
         + last_q_in[...].astype(f32)
@@ -857,7 +953,7 @@
     def _(k):
         spread(q_all, q_sem, k).start()
 
-    lasts()[0].wait_recv()
+    last_feature.wait_recv()
     lane = lax.broadcasted_iota(jnp.int32, (own, 2 * rank), 1)
     feature = [
         total[kind, slot_rows(core), :]
@@ -874,6 +970,8 @@
         feature[1] = feature[1] + curvature_product(turned, in_rows[index])
     primal_ref[...] = feature[0]
     dir_ref[...] = feature[1]
+    for index in (0, 1):
+        outputs(index).start()
 
     @pl.loop(1, columns)
     def _(k):
@@ -884,11 +982,16 @@
     both = jnp.where(
         lane < rank, pltpu.roll(every[:, : 2 * rank], rank, 1), every[:, 2 * rank : 4 * rank]
     )
+    both = both * inv_all[...]
     both_t = both.T.astype(bf16)
     low_t = every[:, 4 * rank :].T.astype(bf16)
-    gate_curve_in[...] = curvature_product(both_t[:rank], x_buf[...])
-    up_curve_in[...] = curvature_product(both_t[rank:], x_buf[...])
     down_curve_out[...] = curvature_product(low_t[:rank], cot_buf[...])
+    outputs(7).start()
+    product = curvature_product(both_t, x_buf[...])
+    gate_curve_in[...] = product[:rank]
+    up_curve_in[...] = product[rank:]
+    for index in (2, 4):
+        outputs(index).start()
 
     for k in range(1, rows):
         square(k).wait_send()
@@ -907,24 +1010,38 @@
     @pl.loop(1, columns)
     def _(k):
         spread(rank_all, rank_all_sem, k).wait_send()
+        spread(inv_all, inv_sem, k).wait_send()
         spread(q_all, q_sem, k).wait_send()
 
-    @pl.loop(0, chunks)
-    def _(c):
-        for g in (mine, others):
-            for path in range(2):
-                for copy in sends(g, c, path, range(6)):
-                    copy.wait_send()
-
-    for copy in pairs() + lasts():
+    for copy in pairs() + [last_feature, last_q]:
         copy.wait_send()
     for side in range(2):
         for k in range(1, 4):
 
             @pl.when(line_valid(side, k))
             def _(side=side, k=k):
-                for kind in range(2):
+                for kind in range(3):
                     line(side, k, kind).wait_send()
+
+    for index in range(8):
+        outputs(index).wait()
+
+
+def handover_kernel(*refs):
+    sources, targets, held, sem = refs[:8], refs[8:16], refs[16:24], refs[24]
+    fetch = [
+        pltpu.make_async_copy(sources[i], held[i], sem.at[0, i]) for i in range(len(sources))
+    ]
+    place = [
+        pltpu.make_async_copy(held[i], targets[i], sem.at[1, i]) for i in range(len(sources))
+    ]
+    for copy in fetch:
+        copy.start()
+    for arrive, leave in zip(fetch, place):
+        arrive.wait()
+        leave.start()
+    for copy in place:
+        copy.wait()
 
 
 def fused(
@@ -953,7 +1070,7 @@
     rank = gate_output_factor.shape[0]
     chunks = hidden // width
     chip, rest, count = 2 * own, 6 * own, 8 * own
-    lead = (3 * chunks) // 7
+    lead, gap = chunks // 2, 2
     half_panel = 3 * width // 2
     f32, bf16 = jnp.float32, jnp.bfloat16
     vmem = pl.BlockSpec(memory_space=pltpu.VMEM)
@@ -971,33 +1088,40 @@
 
     dma = pltpu.SemaphoreType.DMA
     slots, sides = 7, 3
+    shapes = [
+        jax.ShapeDtypeStruct((own, depth), f32),
+        jax.ShapeDtypeStruct((own, depth), f32),
+        jax.ShapeDtypeStruct((rank, depth), f32),
+        jax.ShapeDtypeStruct((rank, hidden), f32),
+        jax.ShapeDtypeStruct((rank, depth), f32),
+        jax.ShapeDtypeStruct((rank, hidden), f32),
+        jax.ShapeDtypeStruct((rank, hidden), f32),
+        jax.ShapeDtypeStruct((rank, depth), f32),
+    ]
     results = pl.pallas_call(
-        functools.partial(lora_kernel, lead),
-        out_shape=[
-            jax.ShapeDtypeStruct((own, depth), f32),
-            jax.ShapeDtypeStruct((own, depth), f32),
-            jax.ShapeDtypeStruct((rank, depth), f32),
-            jax.ShapeDtypeStruct((rank, hidden), f32),
-            jax.ShapeDtypeStruct((rank, depth), f32),
-            jax.ShapeDtypeStruct((rank, hidden), f32),
-            jax.ShapeDtypeStruct((rank, hidden), f32),
-            jax.ShapeDtypeStruct((rank, depth), f32),
-        ],
+        functools.partial(lora_kernel, lead, gap),
+        out_shape=shapes,
         in_specs=[vmem] * 3 + [anywhere] * 15,
-        out_specs=[vmem] * 8,
-        scratch_shapes=[
+        out_specs=[anywhere] * 8,
+        scratch_shapes=[pltpu.VMEM(shape.shape, f32) for shape in shapes]
+        + [
             pltpu.VMEM((count, depth), bf16),
             pltpu.VMEM((count, depth), bf16),
-            pltpu.VMEM((4, own, 128), f32),
+            pltpu.VMEM((4, own, 2 * rank), f32),
             pltpu.VMEM((own, 6 * rank), bf16),
             pltpu.VMEM((4, own, 6 * rank), bf16),
             pltpu.VMEM((count, 6 * rank), bf16),
+            pltpu.VMEM((count, 2 * rank), f32),
             pltpu.VMEM((3, 2 * rank, depth), bf16),
             pltpu.VMEM((3, 2 * rank, hidden), bf16),
             pltpu.VMEM((slots, 2, depth, width), bf16),
             pltpu.VMEM((sides, width, depth), bf16),
         ]
-        + reduce_buffers(chip)
+        + [
+            pltpu.VMEM((chunks, 4, chip // 4, 3 * width), bf16),
+            pltpu.VMEM((chunks, 3, chip // 4, 3 * width), bf16),
+            pltpu.VMEM((chunks, 4, chip // 4, 3 * width), bf16),
+        ]
         + reduce_buffers(rest)
         + [
             pltpu.VMEM((3, 2 * chip, 2 * rank), bf16),
@@ -1031,14 +1155,16 @@
             dma((2, 4)),
             dma((2, 4)),
             dma((2, 8)),
-            dma((chunks, 2, 6)),
-            dma((chunks, 2, 6)),
-            dma((chunks, 2, 6)),
-            dma((chunks, 2, 6)),
+            dma((2, 8)),
+            dma((chunks, 2)),
+            dma((chunks, 2)),
+            dma((chunks, 2)),
+            dma((chunks, 7)),
             dma((2, 2)),
-            dma((2, 2, 3, 2)),
+            dma((2, 2, 3, 3)),
             dma((2, 2)),
             dma((2, 8)),
+            dma((8,)),
         ],
         compiler_params=pltpu.CompilerParams(
             collective_id=2, has_side_effects=True, vmem_limit_bytes=63 * 1024 * 1024
@@ -1065,7 +1191,14 @@
         down_input_factor_direction.T,
     )
     primal, direction, gate_input, gate_output, up_input, up_output, down_input, down_output = (
-        results
+        pl.pallas_call(
+            handover_kernel,
+            out_shape=shapes,
+            in_specs=[anywhere] * 8,
+            out_specs=[anywhere] * 8,
+            scratch_shapes=[pltpu.VMEM(shape.shape, f32) for shape in shapes] + [dma((2, 8))],
+            name="handover",
+        )(*results)
     )
     return (
         primal,
@@ -1270,7 +1403,7 @@
     if (
         lax.axis_size("row") == 4
         and lax.axis_size("col") == 8
-        and gate_frozen_weight.shape[1] % (7 * width) == 0
+        and gate_frozen_weight.shape[1] % (14 * width) == 0
         and gate_frozen_weight.shape[0] % 128 == 0
         and gate_input_factor.shape[1] == 64
         and tokens.shape[0] % 32 == 0

time: 170 us -> 150 us (0.88)
  local copies, waits for them, and re-layouts: 15.5 us -> 0 us
  Pallas kernels: 153 us -> 149 us
    unnamed x8 -> x0, local copies, waits for them, and re-layouts: 15.5 us -> none
    pallas_call x1 -> x2, Pallas kernels: 153 us -> 149 us  [the longest x1 145 us: fused(): pl.pallas_call(functools.partial(lora_kernel, lead, gap), out_shape=shape...]
where the time goes in v2:
time: 150 us
  Pallas kernels  149 us (99%)
    pallas_call x1, Pallas kernels, fused(): pl.pallas_call(functools.partial(lora_kernel, lead, gap), out_shape=shape...  145 us
    pallas_call x1, Pallas kernels, fused(): pl.pallas_call(handover_kernel, out_shape=shapes, in_specs=[anywhere] * 8...  4.44 us

profile of v2, /device:TPU:0, one launch (start us, length us, event | category | flops | bytes accessed | tf_op | source)
XLA Modules:
  0.0 150.1 jit_solution(9497083002408568441)
XLA Ops:
  0.6 145.0 %lora.1 = (f32[32,2048]{1,0:T(8,128)}, f32[32,2048]{1,0:T(8,128)}, f32[64,2048]{1,0:T(8,128)}, f32[64,3584]{1,0:T(8,128)}, f32[64,2048]{1,0:T(8,128)}, /*index=5...) custom-call(bf16[32,2048]{1,0:T(8,128)(2,1)} %tokens.1, f32[1,2048]{1,0:T(1,128)} %bitcast.16, ...), custom_call_target="tpu_custom_call" | custom-call | tf_op jit(solution)/shard_map/lora/pallas_call | solution.py:1101
  145.7 4.4 %handover.1 = (f32[32,2048]{1,0:T(8,128)}, f32[32,2048]{1,0:T(8,128)}, f32[64,2048]{1,0:T(8,128)}, f32[64,3584]{1,0:T(8,128)}, f32[64,2048]{1,0:T(8,128)}, /*ind...) custom-call(f32[32,2048]{1,0:T(8,128)} %get-tuple-element.24.refs_0_, ...), custom_call_target="tpu_custom_call" | custom-call | tf_op jit(solution)/shard_map/handover/pallas_call | solution.py:1194

commit v3 on v2

--- a/solution.py
+++ b/solution.py
@@ -457,8 +457,6 @@
     for k in range(1, rows):
         rank_row(k).start()
 
-    pass_on(0, 1)
-
     def clear():
         total[...] = jnp.zeros_like(total)
         for ref in (gate_q, up_q, low_q, gate_curve, up_curve, down_curve):
@@ -484,6 +482,9 @@
     def spread_arrival(buffer, sem, k):
         at = buffer.at[slot_rows(slot_from(k))]
         return remote(at, at, sem.at[0, k], sem.at[1, k], col_peer(k))
+
+    partner_step = 7 - 6 * core
+    partner_ahead = 1 + 6 * core
 
     def share_ranks():
         sum_squares = squares[0]
@@ -502,12 +503,17 @@
                 block = block * inv
             rank_all[slot_rows(core), at] = block.astype(bf16)
 
+        spread(rank_all, rank_all_sem, partner_ahead).start()
+        spread(inv_all, inv_sem, partner_ahead).start()
+
+    def spread_ranks():
         @pl.loop(1, columns)
         def _(k):
-            spread(rank_all, rank_all_sem, k).start()
-            spread(inv_all, inv_sem, k).start()
-
-    partner_step = 7 - 6 * core
+            @pl.when(k != partner_ahead)
+            def _():
+                spread(rank_all, rank_all_sem, k).start()
+                spread(inv_all, inv_sem, k).start()
+
 
     class Group:
         pass
@@ -796,7 +802,7 @@
 
                 @pl.when(line_valid(side, k) & ((z == 0) if side == 0 else (z == 3)))
                 def _(side=side, k=k):
-                    line_send(side, k, (0, 1, 2))
+                    line_send(side, k, (2, 0, 1))
 
     def line_stage(k, kinds):
         for side in range(2):
@@ -807,27 +813,30 @@
                     line_arrival(side, k, kind).wait_recv()
                 line_send(side, k, kinds)
 
-    def line_end():
+    def line_end(kinds):
         for side in range(2):
 
             @pl.when(line_fed(side))
             def _(side=side):
-                for kind in range(3):
+                for kind in kinds:
                     line_arrival(side, 0, kind).wait_recv()
 
     turn = lead + chunks
     resume = turn + gap
-    rest_end = turn + 3
+    own_lags = (0, 2, 4)
+    rest_lags = (0, 1, 2, 3, 4)
+    rest_end = turn - 1 + rest_lags[4]
     late = {
         rest_end: exchange,
         rest_end + 1: line_open,
-        rest_end + 3: functools.partial(line_stage, 2, (0,)),
-        rest_end + 4: functools.partial(line_stage, 2, (1, 2)),
-        rest_end + 5: functools.partial(line_stage, 1, (0,)),
-        rest_end + 6: functools.partial(line_stage, 1, (1, 2)),
+        rest_end + 4: functools.partial(line_stage, 2, (2, 0)),
+        rest_end + 5: functools.partial(line_stage, 2, (1,)),
+        rest_end + 6: functools.partial(line_stage, 1, (2, 0)),
+        rest_end + 8: functools.partial(line_stage, 1, (1,)),
     }
-    relays = [(1, 1), (0, 2), (1, 2), (0, 3), (1, 3)]
-    early = max(min(lead - 3, len(relays)), 0)
+    relays = [(0, 1), (1, 1), (0, 2), (1, 2), (0, 3), (1, 3)]
+    relay_at = [1, 3, 4, 5, 6, lead - 1]
+    early = sum(step < lead for step in relay_at)
 
     def share():
         share_ranks()
@@ -860,7 +869,7 @@
     for which in range(2):
         near_arrival(which, 0).wait_recv()
 
-    last_step = steps + gap + 4
+    last_step = steps + gap + own_lags[2]
 
     @pl.loop(0, last_step)
     def _(t):
@@ -886,19 +895,20 @@
                 stage(others, s - lead, s)
 
         at_step(lead, arrive)
-        at_step(4, first_ready)
-        at_step(lead + 4, rest_ready)
-        for lag, stage in enumerate((project, relay, settle, forward, differentiate)):
+        at_step(own_lags[2], first_ready)
+        at_step(lead + 1, spread_ranks)
+        at_step(lead + rest_lags[4], rest_ready)
+        for lag, stage in zip(rest_lags, (project, relay, settle, forward, differentiate)):
             rest_stage(lag, stage)
         for step, action in late.items():
             if step < last_step:
                 at_step(step, action)
         own_stage(0, project)
-        at_step(0, share)
-        own_stage(2, reduce)
-        own_stage(4, differentiate)
+        at_step(2, share)
+        own_stage(own_lags[1], reduce)
+        own_stage(own_lags[2], differentiate)
         for index, (which, k) in enumerate(relays[:early]):
-            at_step(index + 1 + index // 3, functools.partial(pass_on, which, k))
+            at_step(relay_at[index], functools.partial(pass_on, which, k))
 
     for step, action in late.items():
         if step >= last_step:
@@ -939,7 +949,7 @@
         sent_eight(c).wait_send()
         landed_four(c).wait_send()
 
-    line_end()
+    line_end((2,))
     last_q.wait_recv()
     q_own = (
         q_rows(core)
@@ -947,14 +957,21 @@
         + line_q_in[0, 0].astype(f32)
         + line_q_in[1, 0].astype(f32)
     )
-    q_all[slot_rows(core), :] = q_own.astype(bf16)
+    lane = lax.broadcasted_iota(jnp.int32, (own, 2 * rank), 1)
+    both = jnp.where(
+        lane < rank, pltpu.roll(q_own[:, : 2 * rank], rank, 1), q_own[:, 2 * rank : 4 * rank]
+    )
+    q_all[slot_rows(core), : 2 * rank] = (
+        both * inv_all[slot_rows(core), :] * adapter_scale
+    ).astype(bf16)
+    q_all[slot_rows(core), 2 * rank :] = (q_own[:, 4 * rank :] * adapter_scale).astype(bf16)
 
     @pl.loop(1, columns)
     def _(k):
         spread(q_all, q_sem, k).start()
 
+    line_end((0, 1))
     last_feature.wait_recv()
-    lane = lax.broadcasted_iota(jnp.int32, (own, 2 * rank), 1)
     feature = [
         total[kind, slot_rows(core), :]
         + last_in[kind].astype(f32)
@@ -977,14 +994,9 @@
     def _(k):
         spread_arrival(q_all, q_sem, k).wait_recv()
 
-    every = q_all[...].astype(f32) * adapter_scale
-    lane = lax.broadcasted_iota(jnp.int32, (count, 2 * rank), 1)
-    both = jnp.where(
-        lane < rank, pltpu.roll(every[:, : 2 * rank], rank, 1), every[:, 2 * rank : 4 * rank]
-    )
-    both = both * inv_all[...]
-    both_t = both.T.astype(bf16)
-    low_t = every[:, 4 * rank :].T.astype(bf16)
+    every = q_all[...].astype(f32)
+    both_t = every[:, : 2 * rank].T.astype(bf16)
+    low_t = every[:, 2 * rank :].T.astype(bf16)
     down_curve_out[...] = curvature_product(low_t[:rank], cot_buf[...])
     outputs(7).start()
     product = curvature_product(both_t, x_buf[...])
@@ -1070,7 +1082,7 @@
     rank = gate_output_factor.shape[0]
     chunks = hidden // width
     chip, rest, count = 2 * own, 6 * own, 8 * own
-    lead, gap = chunks // 2, 2
+    lead, gap = (8 * chunks) // 14, 3
     half_panel = 3 * width // 2
     f32, bf16 = jnp.float32, jnp.bfloat16
     vmem = pl.BlockSpec(memory_space=pltpu.VMEM)
@@ -1144,7 +1156,7 @@
             pltpu.VMEM((2, own, depth), bf16),
             pltpu.VMEM((own, 6 * rank), bf16),
             pltpu.VMEM((own, 6 * rank), bf16),
-            pltpu.VMEM((count, 6 * rank), bf16),
+            pltpu.VMEM((count, 4 * rank), bf16),
             dma((12,)),
             dma((slots, 2)),
             dma((sides,)),

time: 150 us -> 141 us (0.940)
  Pallas kernels: 149 us -> 140 us
    pallas_call x1, Pallas kernels: 145 us -> 136 us  [fused(): pl.pallas_call(functools.partial(lora_kernel, lead, gap), out_shape=shape...]
where the time goes in v3:
time: 141 us
  Pallas kernels  140 us (99%)
    pallas_call x1, Pallas kernels, fused(): pl.pallas_call(functools.partial(lora_kernel, lead, gap), out_shape=shape...  136 us
    pallas_call x1, Pallas kernels, fused(): pl.pallas_call(handover_kernel, out_shape=shapes, in_specs=[anywhere] * 8...  4.44 us

profile of v3, /device:TPU:0, one launch (start us, length us, event | category | flops | bytes accessed | tf_op | source)
XLA Modules:
  0.0 140.6 jit_solution(13714659830113377771)
XLA Ops:
  0.6 135.5 %lora.1 = (f32[32,2048]{1,0:T(8,128)}, f32[32,2048]{1,0:T(8,128)}, f32[64,2048]{1,0:T(8,128)}, f32[64,3584]{1,0:T(8,128)}, f32[64,2048]{1,0:T(8,128)}, /*index=5...) custom-call(bf16[32,2048]{1,0:T(8,128)(2,1)} %tokens.1, f32[1,2048]{1,0:T(1,128)} %bitcast.16, ...), custom_call_target="tpu_custom_call" | custom-call | tf_op jit(solution)/shard_map/lora/pallas_call | solution.py:1113
  136.2 4.4 %handover.1 = (f32[32,2048]{1,0:T(8,128)}, f32[32,2048]{1,0:T(8,128)}, f32[64,2048]{1,0:T(8,128)}, f32[64,3584]{1,0:T(8,128)}, f32[64,2048]{1,0:T(8,128)}, /*ind...) custom-call(f32[32,2048]{1,0:T(8,128)} %get-tuple-element.24.refs_0_, ...), custom_call_target="tpu_custom_call" | custom-call | tf_op jit(solution)/shard_map/handover/pallas_call | solution.py:1206

commit v4 on v3

--- a/solution.py
+++ b/solution.py
@@ -835,7 +835,7 @@
         rest_end + 8: functools.partial(line_stage, 1, (1,)),
     }
     relays = [(0, 1), (1, 1), (0, 2), (1, 2), (0, 3), (1, 3)]
-    relay_at = [1, 3, 4, 5, 6, lead - 1]
+    relay_at = [2, 3, 4, 5, 6, lead - 1]
     early = sum(step < lead for step in relay_at)
 
     def share():

time: 141 us -> 140 us (level)
  no operation moved by 1% of the time
where the time goes in v4:
time: 140 us
  Pallas kernels  140 us (100%)
    pallas_call x1, Pallas kernels, fused(): pl.pallas_call(functools.partial(lora_kernel, lead, gap), out_shape=shape...  135 us
    pallas_call x1, Pallas kernels, fused(): pl.pallas_call(handover_kernel, out_shape=shapes, in_specs=[anywhere] * 8...  4.44 us

profile of v4, /device:TPU:0, one launch (start us, length us, event | category | flops | bytes accessed | tf_op | source)
XLA Modules:
  0.0 140.3 jit_solution(938103417055061295)
XLA Ops:
  0.6 135.2 %lora.1 = (f32[32,2048]{1,0:T(8,128)}, f32[32,2048]{1,0:T(8,128)}, f32[64,2048]{1,0:T(8,128)}, f32[64,3584]{1,0:T(8,128)}, f32[64,2048]{1,0:T(8,128)}, /*index=5...) custom-call(bf16[32,2048]{1,0:T(8,128)(2,1)} %tokens.1, f32[1,2048]{1,0:T(1,128)} %bitcast.16, ...), custom_call_target="tpu_custom_call" | custom-call | tf_op jit(solution)/shard_map/lora/pallas_call | solution.py:1113
  135.8 4.4 %handover.1 = (f32[32,2048]{1,0:T(8,128)}, f32[32,2048]{1,0:T(8,128)}, f32[64,2048]{1,0:T(8,128)}, f32[64,3584]{1,0:T(8,128)}, f32[64,2048]{1,0:T(8,128)}, /*ind...) custom-call(f32[32,2048]{1,0:T(8,128)} %get-tuple-element.24.refs_0_, ...), custom_call_target="tpu_custom_call" | custom-call | tf_op jit(solution)/shard_map/handover/pallas_call | solution.py:1206
